TPU v7x, 128 devices: a whole 4x4x4 slice. The times are simulated.
128 devices in a mesh: ctx: 32 (over y, z, core), fsdp: 4 (over x).
Axes of the slice: x: 4, y: 4, z: 4, core: 2. Of those that a mesh axis runs over, the one named last changes fastest.
Arguments:
- gate_in: bfloat16 [16384, 4096], P('ctx', 'fsdp'), may hold values from -6 to 6
- values: bfloat16 [16384, 4096], P('ctx', 'fsdp'), may hold values from -6 to 6
- gate_out: bfloat16 [16384, 4096], P('ctx', 'fsdp'), may hold values from -6 to 6
- bias: float32 [4096], P('fsdp'), may hold values from -4 to 4
- spectrum: bfloat16 [2, 32768, 4096], P(None, ('ctx', 'fsdp')), may hold values from -6 to 6
Outputs:
- gated: bfloat16 [16384, 4096], P('ctx', 'fsdp')
All inputs are finite; a program needn't handle non-finite values.
Results may differ from a plain program's by a relative error of at most 0.0049.
Values may be sent and summed in bfloat16 or wider, within the bound.
No kernel may reach another device: no remote copies, remote signals or barrier semaphores. Data moves between devices by JAX's collectives and lax.ppermute only.
A program may use at most 128 MiB of HBM per device.

v0:
```python
import math

import jax
import jax.numpy as jnp
from jax import lax
from jax.sharding import PartitionSpec as P


def phase_angles(rows_side, cols_side, modulus):
    product = rows_side[:, None] * cols_side[None, :] % modulus
    return product.astype(jnp.float32) * (2.0 * math.pi / modulus)


def contract(matrix, operand):
    return jnp.einsum("kj,sjc->skc", matrix, operand, precision=lax.Precision.HIGHEST)


def mix_rows(matrix, operand):
    return jnp.einsum("kp,pjc->kjc", matrix, operand, precision=lax.Precision.HIGHEST)


def body(gate_in, values, gate_out, bias, spectrum):
    devices = lax.axis_size("ctx")
    rows_here = gate_in.shape[0]
    channels = gate_in.shape[1]
    block_rows = rows_here // devices
    length_total = 2 * rows_here * devices
    position = lax.axis_index("ctx")
    mixed = (gate_in.astype(jnp.float32) * values.astype(jnp.float32)).astype(jnp.bfloat16)
    mixed = lax.optimization_barrier(mixed)
    member = lax.axis_index("fsdp")
    filter_here = lax.dynamic_slice_in_dim(
        lax.all_gather(spectrum, "fsdp", axis=1, tiled=True), member * channels, channels, 2
    )
    source_index = jnp.arange(devices, dtype=jnp.int32)
    mirror_index = jnp.where(source_index == 0, devices, 2 * devices - source_index)
    radix_order = jnp.stack([source_index, mirror_index], axis=1).reshape(2 * devices)
    cross_angle = phase_angles(radix_order, source_index, 2 * devices)
    cross_cos = jnp.cos(cross_angle)
    cross_sin = jnp.sin(cross_angle)
    local_rows = position * block_rows + jnp.arange(block_rows, dtype=jnp.int32)
    twist_angle = (radix_order[:, None] * local_rows[None, :] % length_total).astype(
        jnp.float32
    ) * (2.0 * math.pi / length_total)
    twist_cos = jnp.cos(twist_angle)[:, :, None]
    twist_sin = jnp.sin(twist_angle)[:, :, None]
    source = mixed[None]
    width_now = source.shape[2]
    real_in = lax.all_to_all(
        source.reshape(source.shape[0], devices, block_rows, width_now),
        "ctx",
        split_axis=1,
        concat_axis=1,
        tiled=True,
    )[0].astype(jnp.float32)
    real_mix = mix_rows(cross_cos, real_in)
    imag_mix = -mix_rows(cross_sin, real_in)
    spread = jnp.stack(
        [real_mix * twist_cos + imag_mix * twist_sin, imag_mix * twist_cos - real_mix * twist_sin]
    )
    regrouped = lax.all_to_all(spread, "ctx", split_axis=1, concat_axis=2, tiled=True)
    row_index = jnp.arange(rows_here, dtype=jnp.int32)
    local_angle = phase_angles(row_index, row_index, rows_here)
    local_cos = jnp.cos(local_angle)
    local_sin = jnp.sin(local_angle)
    real_part = regrouped[0]
    imag_part = regrouped[1]
    freq_real = contract(local_cos, real_part) + contract(local_sin, imag_part)
    freq_imag = contract(local_cos, imag_part) - contract(local_sin, real_part)
    filter_float = filter_here.astype(jnp.float32).reshape(2, 2, rows_here, channels)
    prod_real = freq_real * filter_float[0] - freq_imag * filter_float[1]
    prod_imag = freq_real * filter_float[1] + freq_imag * filter_float[0]
    back_real = contract(local_cos, prod_real) - contract(local_sin, prod_imag)
    back_imag = contract(local_cos, prod_imag) + contract(local_sin, prod_real)
    pair_index = jnp.stack([position, jnp.where(position == 0, devices, 2 * devices - position)])
    back_angle = (pair_index[:, None] * row_index[None, :] % length_total).astype(jnp.float32) * (
        2.0 * math.pi / length_total
    )
    back_cos = jnp.cos(back_angle)[:, :, None]
    back_sin = jnp.sin(back_angle)[:, :, None]
    turned_real = back_real * back_cos - back_imag * back_sin
    turned_imag = back_real * back_sin + back_imag * back_cos
    stacked = jnp.stack([turned_real, turned_imag]).reshape(2, 2, devices, block_rows, width_now)
    inverse_angle = phase_angles(source_index, radix_order, 2 * devices)
    inverse_cos = jnp.cos(inverse_angle) / length_total
    inverse_sin = jnp.sin(inverse_angle) / length_total
    received = lax.all_to_all(stacked, "ctx", split_axis=2, concat_axis=1, tiled=True)
    real_block = received[0, :, 0]
    imag_block = received[1, :, 0]
    real_out = mix_rows(inverse_cos, real_block) - mix_rows(inverse_sin, imag_block)
    folded = real_out[None]
    restored = lax.all_to_all(folded, "ctx", split_axis=1, concat_axis=1, tiled=True)
    restored = restored.reshape(restored.shape[0], rows_here, width_now)
    convolved_part = restored[0]
    convolved = convolved_part + bias[None, :] * mixed.astype(jnp.float32)
    return (gate_out.astype(jnp.float32) * convolved).astype(jnp.bfloat16)


def solution(mesh):
    return jax.shard_map(
        body,
        mesh=mesh,
        in_specs=(
            P("ctx", "fsdp"),
            P("ctx", "fsdp"),
            P("ctx", "fsdp"),
            P("fsdp"),
            P(None, ("ctx", "fsdp"), None),
        ),
        out_specs=P("ctx", "fsdp"),
        check_vma=False,
    )
```

profile of v0, /device:TPU:1, one launch (start us, length us, event | category | flops | bytes accessed | tf_op | source)
XLA Modules:
  0.0 493.6 jit_solution(11693524858831694724)
XLA Ops:
  6.5 0.0 copy-start.1
  6.5 0.0 copy-start.2
  6.5 0.0 all-gather.2.cloned.1.call-start
  6.5 0.7 all-gather.2.cloned.1.call-update
  7.3 0.5 copy-done.1
  7.8 0.3 copy-done.2
  8.1 1.4 multiply_convert_fusion
  9.4 9.6 %all-to-all-start = ((bf16[1,32,16,1024]{3,2,0,1:T(8,128)(2,1)}), bf16[1,32,16,1024]{3,2,0,1:T(8,128)(2,1)S(1)}, u32[]{:S(2)}, u32[]{:S(2)}) async-start(bf16[1,32,16,1024]{3,2,0,1:T(8,128)(2,1)} %bitcast.3), calls=%async_computation | async-start | bytes 2097152 | tf_op jit(solution)/shard_map/all_to_all | solution.py:49
  19.1 0.1 copy.52
  19.2 0.1 mul.274
  19.3 0.1 fusion.79
  19.4 16.5 %all-to-all-done = bf16[1,32,16,1024]{3,2,0,1:T(8,128)(2,1)S(1)} async-done(((bf16[1,32,16,1024]{3,2,0,1:T(8,128)(2,1)}), bf16[1,32,16,1024]{3,2,0,1:T(8,128)(2,1)S(1)}, u32[]{:S(2)}, u32[]{:S(2)}) %all-to-all-start) | async-done | bytes 1048608 | tf_op jit(solution)/shard_map/all_to_all | solution.py:49
  36.0 2.7 fusion.25
  38.6 3.6 add_bitcast_fusion
  42.2 1.7 pad_maximum_fusion
  43.9 8.3 %copy.55 = f32[2,64,16,1024]{3,2,0,1:T(8,128)} copy(f32[2,64,16,1024]{3,1,2,0:T(8,128)S(1)} %pad_maximum_fusion) | data formatting | bytes 16777216 | tf_op jit(solution)/shard_map/stack | solution.py:58
  52.1 4.8 all-to-all-start.1
  56.9 0.1 pad_add_fusion.1
  57.0 0.2 fusion.81
  57.2 104.1 %all-to-all-done.1 = f32[2,64,16,1024]{3,2,0,1:T(8,128)} async-done(((f32[2,64,16,1024]{3,2,0,1:T(8,128)}), f32[2,64,16,1024]{3,2,0,1:T(8,128)}, u32[]{:S(2)}, u32[]{:S(2)}) %all-to-all-start.1) | async-done | bytes 8388640 | tf_op jit(solution)/shard_map/all_to_all | solution.py:61
  161.3 4.2 copy.56
  165.5 1.7 fusion.134
  167.1 0.5 copy.57
  167.7 0.0 copy-start
  167.7 0.5 copy.59
  168.2 1.4 copy-done
  169.7 17.0 %fusion.23 = f32[2,1024,512]{2,1,0:T(8,128)S(1)} fusion(f32[2,512,1024]{2,1,0:T(8,128)S(1)} %bitcast.102), kind=kOutput, calls=%fused_computation.42 | convolution fusion | flops 6446120960 | bytes 8388608 | tf_op jit(solution)/shard_map/kj,sjc->skc/dot_general | solution.py:15
  186.7 18.7 %fusion.21 = f32[2,1024,512]{2,1,0:T(8,128)} fusion(f32[2,512,1024]{2,1,0:T(8,128)S(1)} %bitcast.100), kind=kOutput, calls=%fused_computation.40 | convolution fusion | flops 6446120960 | bytes 8388608 | tf_op jit(solution)/shard_map/kj,sjc->skc/dot_general | solution.py:15
  205.4 18.5 %convolution_add_fusion.1 = f32[2,1024,512]{2,1,0:T(8,128)} fusion(f32[2,1024,512]{2,1,0:T(8,128)S(1)} %fusion.23, f32[2,512,1024]{2,1,0:T(8,128)S(1)} %bitcast.101), kind=kOutput, calls=%fused_computation.20 | convolution fusion | flops 6447169536 | bytes 12582912 | tf_op jit(solution)/shard_map/kj,sjc->skc/dot_general | solution.py:15
  223.9 0.0 all-gather.2.cloned.1.call-done
  223.9 3.2 dynamic-slice_convert_fusion
  227.1 4.1 fusion.133
  231.2 5.4 %copy.64 = f32[2,512,1024]{1,2,0:T(8,128)} copy(f32[2,512,1024]{2,1,0:T(8,128)} %bitcast.108) | data formatting | bytes 8388608 | tf_op jit(solution)/shard_map/squeeze | solution.py:71
  236.6 5.4 %copy.61 = f32[2,512,1024]{1,2,0:T(8,128)} copy(f32[2,512,1024]{2,1,0:T(8,128)} %bitcast.107) | data formatting | bytes 8388608 | tf_op jit(solution)/shard_map/squeeze | solution.py:71
  242.1 26.0 %fusion.4 = (f32[2,512,1024]{1,2,0:T(8,128)S(1)}, f32[2,512,1024]{1,2,0:T(8,128)S(1)}) fusion(f32[2,512,1024]{1,2,0:T(8,128)} %copy.64, f32[2,512,1024]{1,2,0:T(8,128)} %copy.61, f32[2,1024,512]{2,1,0:T(8,128)} %convolution_add_fusion.1, f32[2,1024,512]{2,1,0:T(8,128)} %fusion.21, f32[2,512,1024]{2,1,0:T(8,128)} %bitcast.103), kind=kOutput, calls=%fused_computation.8 | convolution fusion | flops 6453460992 | bytes 29360128 | tf_op jit(solution)/shard_map/kj,sjc->skc/dot_general | solution.py:15
  268.0 10.7 %fusion.19 = f32[2,1024,512]{1,2,0:T(8,128)S(1)} fusion(f32[2,512,1024]{1,2,0:T(8,128)S(1)} %get-tuple-element.5), kind=kOutput, calls=%fused_computation.38 | convolution fusion | flops 6446120960 | bytes 8388608 | tf_op jit(solution)/shard_map/kj,sjc->skc/dot_general | solution.py:15
  278.7 11.1 %fusion.17 = f32[2,1024,512]{1,2,0:T(8,128)S(1)} fusion(f32[2,512,1024]{1,2,0:T(8,128)S(1)} %get-tuple-element.6), kind=kOutput, calls=%fused_computation.36 | convolution fusion | flops 6446120960 | bytes 8388608 | tf_op jit(solution)/shard_map/kj,sjc->skc/dot_general | solution.py:15
  289.8 11.2 %convolution_subtract_fusion = f32[2,1024,512]{1,2,0:T(8,128)S(1)} fusion(f32[2,1024,512]{1,2,0:T(8,128)S(1)} %fusion.19, f32[2,512,1024]{1,2,0:T(8,128)S(1)} %get-tuple-element.6), kind=kOutput, calls=%fused_computation.18 | convolution fusion | flops 6447169536 | bytes 12582912 | tf_op jit(solution)/shard_map/kj,sjc->skc/dot_general | solution.py:15
  301.0 12.2 %multiply_subtract_fusion = (f32[2,1024,512]{1,2,0:T(8,128)S(1)}, f32[2,1024,512]{1,2,0:T(8,128)S(1)}) fusion(f32[2,1024,512]{1,2,0:T(8,128)S(1)} %convolution_subtract_fusion, f32[2,512]{1,0:T(2,128)S(1)} %get-tuple-element.20, f32[2,512]{1,0:T(2,128)S(1)} %get-tuple-element.19, f32[2,1024,512]{1,2,0:T(8,128)S(1)} %fusion.17, ...), kind=kOutput, calls=%fused_computation.13 | convolution fusion | flops 6453460992 | bytes 20979712 | tf_op jit(solution)/shard_map/kj,sjc->skc/dot_general | solution.py:15
  313.2 1.7 pad_maximum_fusion.1
  314.9 1.7 copy.84
  316.6 123.0 %all_to_all.40 = f32[2,2,32,16,1024]{4,3,1,0,2:T(8,128)S(1)} all-to-all(f32[2,2,32,16,1024]{4,3,1,0,2:T(8,128)S(1)} %copy.84), channel_id=1, replica_groups=mesh['ctx'=32,'fsdp'=4] {'ctx'}, dimensions={2} | all-to-all | bytes 16777216 | tf_op jit(solution)/shard_map/all_to_all | solution.py:87
  439.6 1.7 fusion.132
  441.2 4.6 fusion
  445.9 4.7 subtract_bitcast_fusion.1
  450.6 0.0 copy-start.3
  450.6 0.0 copy-start.4
  450.6 1.2 copy.75
  451.8 31.8 %all_to_all.41 = f32[1,32,16,1024]{3,2,0,1:T(8,128)S(1)} all-to-all(f32[1,32,16,1024]{3,2,0,1:T(8,128)S(1)} %copy.75), channel_id=1, replica_groups=mesh['ctx'=32,'fsdp'=4] {'ctx'}, dimensions={1} | all-to-all | bytes 4194304 | tf_op jit(solution)/shard_map/all_to_all | solution.py:92
  483.7 0.0 copy-done.3
  483.7 0.0 copy-done.4
  483.7 2.9 fusion.7
  (4 shorter events, 0.0 us)
Async XLA Ops:
  6.5 1.2 copy-start.1
  6.5 1.5 copy-start.2
  6.5 217.4 %all-gather.2.cloned.1.call-start = ((), (), s32[]{:S(2)}) async-start(), calls=%async_computation.4 | async-start | bytes 20971520 | tf_op jit(solution)/shard_map/all_gather | solution.py:33
  9.4 26.5 %all-to-all-start = ((bf16[1,32,16,1024]{3,2,0,1:T(8,128)(2,1)}), bf16[1,32,16,1024]{3,2,0,1:T(8,128)(2,1)S(1)}, u32[]{:S(2)}, u32[]{:S(2)}) async-start(bf16[1,32,16,1024]{3,2,0,1:T(8,128)(2,1)} %bitcast.3), calls=%async_computation | async-start | bytes 2097152 | tf_op jit(solution)/shard_map/all_to_all | solution.py:49
  52.1 109.1 %all-to-all-start.1 = ((f32[2,64,16,1024]{3,2,0,1:T(8,128)}), f32[2,64,16,1024]{3,2,0,1:T(8,128)}, u32[]{:S(2)}, u32[]{:S(2)}) async-start(f32[2,64,16,1024]{3,2,0,1:T(8,128)} %copy.55), calls=%async_computation.1 | async-start | bytes 16777216 | tf_op jit(solution)/shard_map/all_to_all | solution.py:61
  167.7 2.0 copy-start
  450.6 33.1 %copy-start.3 = (bf16[512,1024]{1,0:T(8,128)(2,1)S(1)}, bf16[512,1024]{1,0:T(8,128)(2,1)}, u32[]{:S(2)}) copy-start(bf16[512,1024]{1,0:T(8,128)(2,1)} %param.7) | copy-start | bytes 3145732
  450.6 33.1 %copy-start.4 = (f32[1024]{0:T(1024)S(1)}, f32[1024]{0:T(1024)}, u32[]{:S(2)}) copy-start(f32[1024]{0:T(1024)} %param.8) | copy-start | bytes 12292
Sparse Core Ops, SparseCore 0:
  9.0 157.0 all-gather.1
where the time goes:
time: 503 us; the launch traced here: 494 us
  blocking collectives  155 us (31%)
  matrix products  141 us (28%)
  waiting for transfers between devices  121 us (24%)
  local copies, waits for them, and re-layouts  37.1 us (7%)
  starting transfers between devices  14.4 us (3%)
  between operations  13.8 us (3%)
  other arithmetic  11.1 us (2%)
    dot_general x8, matrix products, contract(): jnp.einsum('kj,sjc->skc', matrix, operand, precision=lax.Precision.HIGHEST)  125 us
    all_to_all x1, blocking collectives, body(): lax.all_to_all(stacked, 'ctx', split_axis=2, concat_axis=1, tiled=True)  123 us
    all_to_all x1, waiting for transfers between devices, body(): lax.all_to_all(spread, 'ctx', split_axis=1, concat_axis=2, tiled=True)  104 us
    all_to_all x1, blocking collectives, body(): lax.all_to_all(folded, 'ctx', split_axis=1, concat_axis=1, tiled=True)  31.8 us
    all_to_all x1, waiting for transfers between devices, body(): lax.all_to_all(source.reshape(source.shape[0], devices, block_rows, width...  16.5 us
    dot_general x4, matrix products, mix_rows(): jnp.einsum('kp,pjc->kjc', matrix, operand, precision=lax.Precision.HIGHEST)  15.6 us
    squeeze x2, local copies, waits for them, and re-layouts, body(): prod_real = freq_real * filter_float[0] - freq_imag * filter_float[1]  10.8 us
  transfers between devices with their start and end apart: 3, of which 2 were waited for; matrix products, arithmetic and copies ran while one was open for 16% of the time, Pallas kernels for 0%

commit v1 on v0

v1 whole, which is shorter than its diff:
```python
import functools
import math

import jax
import jax.numpy as jnp
from jax import lax
from jax.experimental import pallas as pl
from jax.experimental.pallas import tpu as pltpu
from jax.sharding import PartitionSpec as P

CHUNKS = 1
LANES = 256


def cosine(step, modulus):
    half = modulus // 2
    centred = jnp.bitwise_and(step + half, modulus - 1) - half
    y = (modulus // 4 - jnp.abs(centred)).astype(jnp.float32) * (2.0 * math.pi / modulus)
    z = y * y
    series = 1.0 / 6227020800.0
    for term in (-1.0 / 39916800.0, 1.0 / 362880.0, -1.0 / 5040.0, 1.0 / 120.0, -1.0 / 6.0, 1.0):
        series = series * z + term
    return series * y


def split(table):
    high = lax.reduce_precision(table, 8, 7)
    return high.astype(jnp.bfloat16), (table - high).astype(jnp.bfloat16)


def cross_table(devices, block, transpose, scale):
    wide = jnp.arange(2 * devices * block, dtype=jnp.int32)
    residue, part, wide_row = wide // (2 * block), (wide // block) % 2, wide % block
    narrow = jnp.arange(devices * block, dtype=jnp.int32)
    place, narrow_row = narrow // block, narrow % block
    first = residue == 0
    rate = jnp.where(first, part * devices, residue)
    phase = jnp.where(first, 0, part * (devices // 2))
    if transpose:
        step = place[:, None] * rate[None, :] + phase[None, :]
        same = narrow_row[:, None] == wide_row[None, :]
    else:
        step = rate[:, None] * place[None, :] + phase[:, None]
        same = wide_row[:, None] == narrow_row[None, :]
    return split(jnp.where(same, cosine(step, 2 * devices) * scale, 0.0))


def local_table(position, devices, rows, block, transpose):
    length = 2 * devices * rows
    stride = 2 * devices
    half = rows // 2
    first = position == 0
    out = jnp.arange(2 * rows, dtype=jnp.int32)
    out_part, order = out // rows, out % rows
    upper = (order >= half).astype(jnp.int32)
    packed_rate = jnp.where(
        order == 0, out_part * half * stride, stride * (order - upper * half) + upper * devices
    )
    rate = jnp.where(first, packed_rate, stride * order + position)
    out_phase = jnp.where(first & (order == 0), 0, out_part)
    inp = jnp.arange(2 * rows, dtype=jnp.int32)
    in_part = (inp // block) % 2
    row = (inp // (2 * block)) * block + inp % block
    in_phase = jnp.where(first, 0, in_part)
    out_side = jnp.where(first, upper, 2)
    quarter = length // 4
    if transpose:
        step = row[:, None] * rate[None, :] + quarter * (out_phase[None, :] - in_phase[:, None])
        keep = (out_side[None, :] == 2) | (out_side[None, :] == in_part[:, None])
    else:
        step = rate[:, None] * row[None, :] + quarter * (out_phase[:, None] - in_phase[None, :])
        keep = (out_side[:, None] == 2) | (out_side[:, None] == in_part[None, :])
    return split(jnp.where(keep, cosine(step, length), 0.0))


def filter_tables(position, member, members, rows):
    first = position == 0
    half = rows // 2
    out = jnp.arange(rows + 8, dtype=jnp.int32)
    order = jnp.minimum(out, rows - 1)
    body = out < rows
    upper = order >= half
    here = jnp.where(first, jnp.where(upper, rows + order - half, order), order)
    there = jnp.where(
        first,
        jnp.where(upper, 2 * rows - 1 - (order - half), (rows - order) % rows),
        2 * rows - 1 - order,
    )
    edge = first & (order == 0)
    stored = jnp.arange(2 * rows, dtype=jnp.int32)
    part = 2 * rows // members
    stored = (member + members - stored // part) % members * part + stored % part
    hit_here = (stored[None, :] == here[:, None]).astype(jnp.float32)
    hit_there = (stored[None, :] == there[:, None]).astype(jnp.float32)
    weight = jnp.where(edge, 0.25, 0.5)[:, None]
    even = weight * (hit_here + hit_there)
    odd = weight * (hit_here - hit_there)
    fix = 0.5 * ((stored[None, :] == half).astype(jnp.float32) - (stored[None, :] == 0).astype(jnp.float32))
    fix = jnp.where(first & (out[:, None] == rows), fix, 0.0)
    even = jnp.where(body[:, None], even, fix)
    return even.astype(jnp.bfloat16), odd[:rows].astype(jnp.bfloat16)


def dot(a, b):
    return jnp.dot(a, b, preferred_element_type=jnp.float32)


def cross_kernel(high_ref, low_ref, x_ref, o_ref):
    x = x_ref[...]
    o_ref[...] = (dot(high_ref[...], x) + dot(low_ref[...], x)).astype(o_ref.dtype)


def filter_kernel(even_ref, odd_ref, *refs):
    *pieces, even_out, odd_out = refs
    rows = pieces[0].shape[1]
    even = odd = 0.0
    for shift, piece in enumerate(pieces):
        cols = slice(shift * rows, (shift + 1) * rows)
        even += dot(even_ref[:, cols], piece[0])
        odd += dot(odd_ref[:, cols], piece[1])
    even_out[...] = even
    odd_out[...] = odd


def local_kernel(fh_ref, fl_ref, gh_ref, gl_ref, even_ref, odd_ref, x_ref, o_ref):
    rows = odd_ref.shape[0]
    x = x_ref[...]
    freq = dot(fh_ref[...], x) + dot(fl_ref[...], x)
    real, imag = freq[:rows], freq[rows:]
    even, odd = even_ref[:rows], odd_ref[...]
    prod_real = real * even - imag * odd
    prod_imag = real * odd + imag * even
    edge = prod_imag[:8] + imag[:8] * even_ref[rows:]
    prod = jnp.concatenate([prod_real, edge, prod_imag[8:]], axis=0).astype(jnp.bfloat16)
    o_ref[...] = (dot(gh_ref[...], prod) + dot(gl_ref[...], prod)).astype(o_ref.dtype)


def whole(array):
    return pl.BlockSpec(array.shape, lambda i: (0,) * array.ndim)


def columns(shape):
    return pl.BlockSpec(shape[:-1] + (LANES,), lambda i: (0,) * (len(shape) - 1) + (i,))


def call(kernel, tables, streams, outs, name):
    many = isinstance(outs, tuple)
    width = streams[0].shape[-1]
    return pl.pallas_call(
        kernel,
        grid=(width // LANES,),
        in_specs=[whole(t) for t in tables] + [columns(s.shape) for s in streams],
        out_specs=tuple(columns(o.shape) for o in outs) if many else columns(outs.shape),
        out_shape=outs,
        name=name,
    )(*tables, *streams)


def exchange(array):
    return lax.all_to_all(array, "ctx", split_axis=0, concat_axis=0, tiled=True)


def body(gate_in, values, gate_out, bias, spectrum):
    devices = lax.axis_size("ctx")
    members = lax.axis_size("fsdp")
    rows, channels = gate_in.shape
    block = rows // devices
    length = 2 * rows * devices
    width = channels // CHUNKS
    position = lax.axis_index("ctx")
    shape = jax.ShapeDtypeStruct

    def cols(array, c):
        return array[..., c * width : (c + 1) * width]

    mixed = [
        (cols(gate_in, c).astype(jnp.float32) * cols(values, c).astype(jnp.float32)).astype(jnp.bfloat16)
        for c in range(CHUNKS)
    ]
    mixed = lax.optimization_barrier(mixed)
    stage1 = [exchange(m.reshape(devices, block, width)).reshape(rows, width) for m in mixed]

    member = lax.axis_index("fsdp")
    held = []
    for shift in range(members):
        target = lax.rem(member + shift, members)
        piece = lax.dynamic_slice_in_dim(spectrum, target * channels, channels, 2)
        if shift > 0:
            ring = [(m, (m + shift) % members) for m in range(members)]
            piece = lax.ppermute(piece, "fsdp", ring)
        held.append(piece)

    cross = cross_table(devices, block, False, 1.0)
    cross_back = cross_table(devices, block, True, 2.0 / length)
    local = local_table(position, devices, rows, block, False)
    local_back = local_table(position, devices, rows, block, True)
    even_table, odd_table = filter_tables(position, member, members, rows)
    even, odd = call(
        filter_kernel,
        (even_table, odd_table),
        held,
        (shape((rows + 8, channels), jnp.float32), shape((rows, channels), jnp.float32)),
        "filters",
    )

    stage2 = []
    for c in range(CHUNKS):
        spread = call(cross_kernel, cross, (stage1[c],), shape((2 * rows, width), jnp.bfloat16), "cross")
        stage2.append(exchange(spread.reshape(devices, 2 * block, width)).reshape(2 * rows, width))
    stage3 = []
    for c in range(CHUNKS):
        turned = call(
            local_kernel,
            local + local_back,
            (cols(even, c), cols(odd, c), stage2[c]),
            shape((2 * rows, width), jnp.bfloat16),
            "local",
        )
        stage3.append(exchange(turned.reshape(devices, 2 * block, width)).reshape(2 * rows, width))
    outs = []
    for c in range(CHUNKS):
        folded = call(cross_kernel, cross_back, (stage3[c],), shape((rows, width), jnp.bfloat16), "fold")
        restored = exchange(folded.reshape(devices, block, width)).reshape(rows, width)
        convolved = restored.astype(jnp.float32) + cols(bias, c)[None, :] * mixed[c].astype(jnp.float32)
        outs.append((cols(gate_out, c).astype(jnp.float32) * convolved).astype(jnp.bfloat16))
    return jnp.concatenate(outs, axis=1)


def solution(mesh):
    return jax.shard_map(
        body,
        mesh=mesh,
        in_specs=(
            P("ctx", "fsdp"),
            P("ctx", "fsdp"),
            P("ctx", "fsdp"),
            P("fsdp"),
            P(None, ("ctx", "fsdp"), None),
        ),
        out_specs=P("ctx", "fsdp"),
        check_vma=False,
    )
```

time: 503 us -> 167 us (0.33); the launches traced: 494 us -> 166 us
  matrix products: 141 us -> 0 us
  blocking collectives: 155 us -> 21.5 us
  waiting for transfers between devices: 121 us -> 40.4 us
  Pallas kernels: 0 us -> 41.6 us
  local copies, waits for them, and re-layouts: 37.1 us -> 7.05 us
  other arithmetic: 11.1 us -> 30.5 us
  between operations: 13.8 us -> 0.15 us
  starting transfers between devices: 14.4 us -> 24.4 us
    dot_general x12 -> x0, matrix products: 141 us -> none  [the longest x8 125 us: contract(): jnp.einsum('kj,sjc->skc', matrix, operand, precision=lax.Precision.HIGHEST)]
    all_to_all x2 -> x1, blocking collectives: 155 us -> 21.5 us  [exchange(): return lax.all_to_all(array, 'ctx', split_axis=0, concat_axis=0, tiled=True)]
    all_to_all x2 -> x3, waiting for transfers between devices: 121 us -> 40.4 us  [exchange(): return lax.all_to_all(array, 'ctx', split_axis=0, concat_axis=0, tiled=True)]
    pallas_call x0 -> x4, Pallas kernels: none -> 41.6 us  [call(): pl.pallas_call(kernel, grid=(width // LANES,), in_specs=[whole(t) for t i...]
    convert_element_type x3 -> x7, other arithmetic: 7.43 us -> 27.5 us  [the longest x3 19.9 us: split(): return (high.astype(jnp.bfloat16), (table - high).astype(jnp.bfloat16))]
    squeeze x2 -> x0, local copies, waits for them, and re-layouts: 10.8 us -> none  [body(): prod_real = freq_real * filter_float[0] - freq_imag * filter_float[1]]
    another operation x3 -> x0, local copies, waits for them, and re-layouts: 10 us -> none  [the longest x1 8.27 us: body(): jnp.stack([real_mix * twist_cos + imag_mix * twist_sin, imag_mix * twist_...]
    slice x5 -> x2, local copies, waits for them, and re-layouts: 8.46 us -> 0.01 us  [filter_tables(): return (even.astype(jnp.bfloat16), odd[:rows].astype(jnp.bfloat16))]
  transfers between devices with their start and end apart: 3 -> 6, of which waited for: 2 -> 3; matrix products, arithmetic and copies ran while one was open for 16% -> 17% of each run, Pallas kernels for 0% -> 8%
where the time goes in v1:
time: 167 us; the launch traced here: 166 us
  Pallas kernels  41.6 us (25%)
  waiting for transfers between devices  40.4 us (24%)
  other arithmetic  30.5 us (18%)
  starting transfers between devices  24.4 us (15%)
  blocking collectives  21.5 us (13%)
  local copies, waits for them, and re-layouts  7.05 us (4%)
    pallas_call x4, Pallas kernels, call(): pl.pallas_call(kernel, grid=(width // LANES,), in_specs=[whole(t) for t i...  41.6 us
    all_to_all x3, waiting for transfers between devices, exchange(): return lax.all_to_all(array, 'ctx', split_axis=0, concat_axis=0, tiled=True)  40.4 us
    all_to_all x1, blocking collectives, exchange(): return lax.all_to_all(array, 'ctx', split_axis=0, concat_axis=0, tiled=True)  21.5 us
    convert_element_type x3, other arithmetic, split(): return (high.astype(jnp.bfloat16), (table - high).astype(jnp.bfloat16))  19.9 us
    all_to_all x3, starting transfers between devices, exchange(): return lax.all_to_all(array, 'ctx', split_axis=0, concat_axis=0, tiled=True)  18.8 us
    ppermute x3, starting transfers between devices, body(): piece = lax.ppermute(piece, 'fsdp', ring)  5.63 us
    dynamic_slice x1, local copies, waits for them, and re-layouts, body(): piece = lax.dynamic_slice_in_dim(spectrum, target * channels, channels, 2)  4.74 us
  transfers between devices with their start and end apart: 6, of which 3 were waited for; matrix products, arithmetic and copies ran while one was open for 17% of the time, Pallas kernels for 8%

profile of v1, /device:TPU:1, one launch (start us, length us, event | category | flops | bytes accessed | tf_op | source)
XLA Modules:
  0.0 165.7 jit_solution(3908354526637428317)
XLA Ops:
  0.0 0.0 copy-start.2
  0.0 0.0 copy-start.3
  0.0 4.7 %constant_dynamic-slice_fusion = (bf16[2,256,1024]{2,1,0:T(8,128)(2,1)}, bf16[2,256,1024]{2,1,0:T(8,128)(2,1)}, bf16[2,256,1024]{2,1,0:T(8,128)(2,1)}, bf16[2,256,1024]{2,1,0:T(8,128)(2,1)}) fusion(bf16[2,256,4096]{2,1,0:T(8,128)(2,1)} %param.9, s32[]{:T(128)S(6)} %select_n.539, s32[]{:T(128)S(6)} %select_n.537, s32[]{:T(128)S(6)} %select_n.536, ...), kind=kLoop, calls=%fused_computation.136 | loop fusion | bytes 8388624 | tf_op jit(solution)/shard_map/dynamic_slice | solution.py:187
  4.7 2.0 %collective-permute-start = (bf16[2,256,1024]{2,1,0:T(8,128)(2,1)}, bf16[2,256,1024]{2,1,0:T(8,128)(2,1)}, u32[]{:S(2)}, u32[]{:S(2)}) collective-permute-start(bf16[2,256,1024]{2,1,0:T(8,128)(2,1)} %get-tuple-element.10), channel_id=1, source_target_pairs={{0,1},{1,2},{2,3},{3,0},{4,5},{5,6},{6,7},{7,4},{8,9},{9,10},{10,1... | collective-permute-start | bytes 3145736 | tf_op jit(solution)/shard_map/ppermute | solution.py:190
  6.8 2.5 %collective-permute-start.1 = (bf16[2,256,1024]{2,1,0:T(8,128)(2,1)}, bf16[2,256,1024]{2,1,0:T(8,128)(2,1)}, u32[]{:S(2)}, u32[]{:S(2)}) collective-permute-start(bf16[2,256,1024]{2,1,0:T(8,128)(2,1)} %get-tuple-element.12), channel_id=1, source_target_pairs={{0,2},{1,3},{2,0},{3,1},{4,6},{5,7},{6,4},{7,5},{8,10},{9,11},{10,... | collective-permute-start | bytes 3145736 | tf_op jit(solution)/shard_map/ppermute | solution.py:190
  9.2 1.2 collective-permute-start.2
  10.4 0.0 copy-done.2
  10.4 0.0 copy-done.3
  10.4 1.4 multiply_convert_fusion
  11.8 9.6 %all-to-all-start = ((bf16[32,16,1024]{2,1,0:T(8,128)(2,1)}), bf16[32,16,1024]{2,1,0:T(8,128)(2,1)S(1)}, u32[]{:S(2)}, u32[]{:S(2)}) async-start(bf16[32,16,1024]{2,1,0:T(8,128)(2,1)} %bitcast), calls=%async_computation | async-start | bytes 2097152 | tf_op jit(solution)/shard_map/all_to_all | solution.py:160
  21.4 0.0 copy-start.5
  21.6 1.8 %select_convert_fusion.even_ref = bf16[520,1024]{1,0:T(8,128)(2,1)} fusion(bf16[1024]{0:T(1024)(128)(2,1)S(1)} %subtract_multiply_fusion, f32[520]{0:T(1024)S(1)} %fusion.54, pred[520]{0:T(1024)(128)(4,1)S(1)} %get-tuple-element.36, pred[520]{0:T(1024)(128)(4,1)S(1)} %get-tuple-element.35, s32[520]{0:T(1024)S(1)} %get-tuple-element.27, s32[1024]{0:T(1024)S(1)} %fusion.32, ...), kind=kLoop, calls=%fused_computation.28 | loop fusion | flops 4259840 | bytes 1078384 | tf_op jit(solution)/shard_map/convert_element_type | solution.py:101
  23.3 1.6 compare_convert_fusion.1
  25.0 0.0 copy-done.5
  25.0 3.4 %fusion.11 = (bf16[1024,512]{1,0:T(8,128)(2,1)}, bf16[1024,512]{1,0:T(8,128)(2,1)}) fusion(s32[1024]{0:T(1024)S(1)} %get-tuple-element.24, s32[512]{0:T(512)S(1)} %get-tuple-element.25, s32[1024]{0:T(1024)S(1)} %compare_select_fusion.1, s32[512]{0:T(512)S(1)} %get-tuple-element.26, s32[1024]{0:T(1024)S(1)} %get-tuple-element.23), kind=kLoop, calls=%fused_computation.32 | loop fusion | flops 15204352 | bytes 2113536 | tf_op jit(solution)/shard_map/convert_element_type | solution.py:28
  28.4 9.9 %all-to-all-done = bf16[32,16,1024]{2,1,0:T(8,128)(2,1)S(1)} async-done(((bf16[32,16,1024]{2,1,0:T(8,128)(2,1)}), bf16[32,16,1024]{2,1,0:T(8,128)(2,1)S(1)}, u32[]{:S(2)}, u32[]{:S(2)}) %all-to-all-start) | async-done | bytes 1048608 | tf_op jit(solution)/shard_map/all_to_all | solution.py:160
  38.3 0.0 copy-start.1
  38.3 1.0 copy-done.1
  39.3 5.8 %cross.1 = bf16[1024,1024]{1,0:T(8,128)(2,1)} custom-call(bf16[1024,512]{1,0:T(8,128)(2,1)} %get-tuple-element.18.high_ref, bf16[1024,512]{1,0:T(8,128)(2,1)} %get-tuple-element.17.low_ref, bf16[512,1024]{1,0:T(8,128)(2,1)} %bitcast.13), custom_call_target="tpu_custom_call" | custom-call | tf_op jit(solution)/shard_map/cross/pallas_call | solution.py:149
  45.1 0.0 slice-start
  45.1 4.7 %all-to-all-start.1 = ((bf16[32,32,1024]{2,1,0:T(8,128)(2,1)}), bf16[32,32,1024]{2,1,0:T(8,128)(2,1)}, u32[]{:S(2)}, u32[]{:S(2)}) async-start(bf16[32,32,1024]{2,1,0:T(8,128)(2,1)} %bitcast.10), calls=%async_computation.1 | async-start | bytes 4194304 | tf_op jit(solution)/shard_map/all_to_all | solution.py:160
  49.8 0.0 slice-done
  49.8 2.9 %fusion.13.odd_ref = bf16[512,1024]{1,0:T(8,128)(2,1)} fusion(f32[520,1024]{1,0:T(8,128)} %get-tuple-element.22, f32[520,1024]{1,0:T(8,128)S(1)} %get-tuple-element.21, f32[512]{0:T(512)S(1)} %slice-done), kind=kLoop, calls=%fused_computation.35 | loop fusion | flops 1572864 | bytes 5244928 | tf_op jit(solution)/shard_map/convert.1
  52.7 12.9 %fusion.1 = (bf16[1024,1024]{1,0:T(8,128)(2,1)}, bf16[1024,1024]{1,0:T(8,128)(2,1)}, bf16[1024,1024]{1,0:T(8,128)(2,1)}, bf16[1024,1024]{1,0:T(8,128)(2,1)}) fusion(s32[1024]{0:T(1024)S(1)} %get-tuple-element.32, s32[1024]{0:T(1024)S(1)} %get-tuple-element.31, s32[1024]{0:T(1024)S(1)} %get-tuple-element.29, s32[1024]{0:T(1024)S(1)} %get-tuple-element.34, ...), kind=kLoop, calls=%fused_computation.5 | loop fusion | flops 67108864 | bytes 8414208 | tf_op jit(solution)/shard_map/convert_element_type | solution.py:28
  65.6 0.0 collective-permute-done.refs_1_
  65.6 0.0 collective-permute-done.1.refs_2_
  65.6 0.0 collective-permute-done.2.refs_3_
  65.6 6.9 %filters.1 = (f32[520,1024]{1,0:T(8,128)}, f32[512,1024]{1,0:T(8,128)}) custom-call(bf16[520,1024]{1,0:T(8,128)(2,1)} %select_convert_fusion.even_ref, bf16[512,1024]{1,0:T(8,128)(2,1)} %fusion.13.odd_ref, bf16[2,256,1024]{2,1,0:T(8,128)(2,1)} %get-tuple-element.11.refs_0_, bf16[2,256,1024]{2,1,0:T(8,128)(2,1)} %collective-permute-done.refs_1_, ...), custom_call_target="tpu_custom_call" | custom-call | tf_op jit(solution)/shard_map/filters/pallas_call | solution.py:149
  72.5 5.6 %all-to-all-done.1 = bf16[32,32,1024]{2,1,0:T(8,128)(2,1)} async-done(((bf16[32,32,1024]{2,1,0:T(8,128)(2,1)}), bf16[32,32,1024]{2,1,0:T(8,128)(2,1)}, u32[]{:S(2)}, u32[]{:S(2)}) %all-to-all-start.1) | async-done | bytes 2097184 | tf_op jit(solution)/shard_map/all_to_all | solution.py:160
  78.2 23.1 %local.1 = bf16[1024,1024]{1,0:T(8,128)(2,1)} custom-call(bf16[1024,1024]{1,0:T(8,128)(2,1)} %get-tuple-element.16.fh_ref, bf16[1024,1024]{1,0:T(8,128)(2,1)} %get-tuple-element.14.fl_ref, bf16[1024,1024]{1,0:T(8,128)(2,1)} %get-tuple-element.15.gh_ref, bf16[1024,1024]{1,0:T(8,128)(2,1)} %get-tuple-element.13.gl_ref, f32[520,1024]{1,0:T(8,128)} %get-tuple-element.7.even_ref, ...), custom_call_target="tpu_custom_call" | custom-call | tf_op jit(solution)/shard_map/local/pallas_call | solution.py:149
  101.3 4.5 %all-to-all-start.2 = ((bf16[32,32,1024]{2,1,0:T(8,128)(2,1)}), bf16[32,32,1024]{2,1,0:T(8,128)(2,1)S(1)}, u32[]{:S(2)}, u32[]{:S(2)}) async-start(bf16[32,32,1024]{2,1,0:T(8,128)(2,1)} %bitcast.12), calls=%async_computation.2 | async-start | bytes 4194304 | tf_op jit(solution)/shard_map/all_to_all | solution.py:160
  105.8 3.6 %fusion.10 = (bf16[512,1024]{1,0:T(8,128)(2,1)}, bf16[512,1024]{1,0:T(8,128)(2,1)}) fusion(s32[1024]{0:T(1024)S(1)} %get-tuple-element.24, s32[1024]{0:T(1024)S(1)} %compare_select_fusion.1, s32[512]{0:T(512)S(1)} %get-tuple-element.25, s32[1024]{0:T(1024)S(1)} %get-tuple-element.23, s32[512]{0:T(512)S(1)} %get-tuple-element.26), kind=kLoop, calls=%fused_computation.31 | loop fusion | flops 15728640 | bytes 2113536 | tf_op jit(solution)/shard_map/convert_element_type | solution.py:28
  109.4 24.9 %all-to-all-done.2 = bf16[32,32,1024]{2,1,0:T(8,128)(2,1)S(1)} async-done(((bf16[32,32,1024]{2,1,0:T(8,128)(2,1)}), bf16[32,32,1024]{2,1,0:T(8,128)(2,1)S(1)}, u32[]{:S(2)}, u32[]{:S(2)}) %all-to-all-start.2) | async-done | bytes 2097184 | tf_op jit(solution)/shard_map/all_to_all | solution.py:160
  134.2 0.0 copy-start
  134.2 1.3 copy-done
  135.5 5.8 %fold.1 = bf16[512,1024]{1,0:T(8,128)(2,1)} custom-call(bf16[512,1024]{1,0:T(8,128)(2,1)} %get-tuple-element.20.high_ref, bf16[512,1024]{1,0:T(8,128)(2,1)} %get-tuple-element.19.low_ref, bf16[1024,1024]{1,0:T(8,128)(2,1)} %bitcast.11), custom_call_target="tpu_custom_call" | custom-call | tf_op jit(solution)/shard_map/fold/pallas_call | solution.py:149
  141.3 0.0 copy-start.4
  141.3 0.0 copy-start.6
  141.3 21.5 %all_to_all.20 = bf16[32,16,1024]{2,1,0:T(8,128)(2,1)S(1)} all-to-all(bf16[32,16,1024]{2,1,0:T(8,128)(2,1)} %bitcast.14), channel_id=1, replica_groups=mesh['ctx'=32,'fsdp'=4] {'ctx'}, dimensions={0} | all-to-all | bytes 2097152 | tf_op jit(solution)/shard_map/all_to_all | solution.py:160
  162.9 0.0 copy-done.4
  162.9 0.0 copy-done.6
  162.9 2.9 %fusion.15 = bf16[512,1024]{1,0:T(8,128)(2,1)} fusion(bf16[512,1024]{1,0:T(8,128)(2,1)} %multiply_convert_fusion, bf16[512,1024]{1,0:T(8,128)(2,1)S(1)} %copy-done.4, bf16[32,16,1024]{2,1,0:T(8,128)(2,1)S(1)} %all_to_all.20, f32[1024]{0:T(1024)S(1)} %copy-done.6), kind=kLoop, calls=%fused_computation.38 | loop fusion | flops 3670016 | bytes 4198400 | tf_op jit(solution)/shard_map/convert_element_type | solution.py:225
  (12 shorter events, 0.1 us)
Async XLA Ops:
  0.0 10.4 %copy-start.2 = (bf16[512,1024]{1,0:T(8,128)(2,1)S(1)}, bf16[512,1024]{1,0:T(8,128)(2,1)}, u32[]{:S(2)}) copy-start(bf16[512,1024]{1,0:T(8,128)(2,1)} %param.6) | copy-start | bytes 3145732
  0.0 10.4 %copy-start.3 = (bf16[512,1024]{1,0:T(8,128)(2,1)S(1)}, bf16[512,1024]{1,0:T(8,128)(2,1)}, u32[]{:S(2)}) copy-start(bf16[512,1024]{1,0:T(8,128)(2,1)} %param.5) | copy-start | bytes 3145732
  4.7 60.9 %collective-permute-start = (bf16[2,256,1024]{2,1,0:T(8,128)(2,1)}, bf16[2,256,1024]{2,1,0:T(8,128)(2,1)}, u32[]{:S(2)}, u32[]{:S(2)}) collective-permute-start(bf16[2,256,1024]{2,1,0:T(8,128)(2,1)} %get-tuple-element.10), channel_id=1, source_target_pairs={{0,1},{1,2},{2,3},{3,0},{4,5},{5,6},{6,7},{7,4},{8,9},{9,10},{10,1... | collective-permute-start | bytes 3145736 | tf_op jit(solution)/shard_map/ppermute | solution.py:190
  6.8 58.9 %collective-permute-start.1 = (bf16[2,256,1024]{2,1,0:T(8,128)(2,1)}, bf16[2,256,1024]{2,1,0:T(8,128)(2,1)}, u32[]{:S(2)}, u32[]{:S(2)}) collective-permute-start(bf16[2,256,1024]{2,1,0:T(8,128)(2,1)} %get-tuple-element.12), channel_id=1, source_target_pairs={{0,2},{1,3},{2,0},{3,1},{4,6},{5,7},{6,4},{7,5},{8,10},{9,11},{10,... | collective-permute-start | bytes 3145736 | tf_op jit(solution)/shard_map/ppermute | solution.py:190
  9.2 56.4 %collective-permute-start.2 = (bf16[2,256,1024]{2,1,0:T(8,128)(2,1)}, bf16[2,256,1024]{2,1,0:T(8,128)(2,1)}, u32[]{:S(2)}, u32[]{:S(2)}) collective-permute-start(bf16[2,256,1024]{2,1,0:T(8,128)(2,1)} %get-tuple-element.9), channel_id=1, source_target_pairs={{0,3},{1,0},{2,1},{3,2},{4,7},{5,4},{6,5},{7,6},{8,11},{9,8},{10,9... | collective-permute-start | bytes 3145736 | tf_op jit(solution)/shard_map/ppermute | solution.py:190
  11.8 26.5 %all-to-all-start = ((bf16[32,16,1024]{2,1,0:T(8,128)(2,1)}), bf16[32,16,1024]{2,1,0:T(8,128)(2,1)S(1)}, u32[]{:S(2)}, u32[]{:S(2)}) async-start(bf16[32,16,1024]{2,1,0:T(8,128)(2,1)} %bitcast), calls=%async_computation | async-start | bytes 2097152 | tf_op jit(solution)/shard_map/all_to_all | solution.py:160
  21.4 3.5 %copy-start.5 = (f32[520]{0:T(1024)}, f32[520]{0:T(1024)S(1)}, u32[]{:S(2)}) copy-start(f32[520]{0:T(1024)S(1)} %fusion.54) | copy-start | bytes 6244
  38.3 1.0 copy-start.1
  45.1 4.7 %slice-start = ((f32[520]{0:T(1024)}), f32[512]{0:T(512)S(1)}, s32[]{:S(2)}) async-start(f32[520]{0:T(1024)} %copy-done.5), calls=%async_computation.4 | async-start | bytes 4096 | tf_op jit(solution)/shard_map/slice | solution.py:101
  45.1 33.1 %all-to-all-start.1 = ((bf16[32,32,1024]{2,1,0:T(8,128)(2,1)}), bf16[32,32,1024]{2,1,0:T(8,128)(2,1)}, u32[]{:S(2)}, u32[]{:S(2)}) async-start(bf16[32,32,1024]{2,1,0:T(8,128)(2,1)} %bitcast.10), calls=%async_computation.1 | async-start | bytes 4194304 | tf_op jit(solution)/shard_map/all_to_all | solution.py:160
  101.3 32.9 %all-to-all-start.2 = ((bf16[32,32,1024]{2,1,0:T(8,128)(2,1)}), bf16[32,32,1024]{2,1,0:T(8,128)(2,1)S(1)}, u32[]{:S(2)}, u32[]{:S(2)}) async-start(bf16[32,32,1024]{2,1,0:T(8,128)(2,1)} %bitcast.12), calls=%async_computation.2 | async-start | bytes 4194304 | tf_op jit(solution)/shard_map/all_to_all | solution.py:160
  134.2 1.3 copy-start
  141.3 21.5 %copy-start.4 = (bf16[512,1024]{1,0:T(8,128)(2,1)S(1)}, bf16[512,1024]{1,0:T(8,128)(2,1)}, u32[]{:S(2)}) copy-start(bf16[512,1024]{1,0:T(8,128)(2,1)} %param.7) | copy-start | bytes 3145732
  141.3 21.5 %copy-start.6 = (f32[1024]{0:T(1024)S(1)}, f32[1024]{0:T(1024)}, u32[]{:S(2)}) copy-start(f32[1024]{0:T(1024)} %param.8) | copy-start | bytes 12292

commit v2 on v1

v2 whole, which is shorter than its diff:
```python
import math

import jax
import jax.numpy as jnp
from jax import lax
from jax.experimental import pallas as pl
from jax.experimental.pallas import tpu as pltpu
from jax.sharding import PartitionSpec as P


LANES = 256
RADIX = 4


def cosine(step, modulus):
    half = modulus // 2
    centred = jnp.bitwise_and(step + half, modulus - 1) - half
    y = (modulus // 4 - jnp.abs(centred)).astype(jnp.float32) * (2.0 * math.pi / modulus)
    z = y * y
    series = 1.0 / 6227020800.0
    for term in (-1.0 / 39916800.0, 1.0 / 362880.0, -1.0 / 5040.0, 1.0 / 120.0, -1.0 / 6.0, 1.0):
        series = series * z + term
    return series * y


def split(table):
    high = lax.reduce_precision(table, 8, 7)
    return high.astype(jnp.bfloat16), (table - high).astype(jnp.bfloat16)


def message(index, block):
    fine = block // RADIX
    return index % fine * RADIX + index // (2 * fine) % RADIX, index // fine % 2


def cross_table(devices, block, transpose, scale):
    wide = jnp.arange(2 * devices * block, dtype=jnp.int32)
    residue = wide // (2 * block)
    wide_row, part = message(wide, block)
    narrow = jnp.arange(devices * block, dtype=jnp.int32)
    place, narrow_row = narrow // block, narrow % block
    first = residue == 0
    rate = jnp.where(first, part * devices, residue)
    phase = jnp.where(first, 0, part * (devices // 2))
    if transpose:
        step = place[:, None] * rate[None, :] + phase[None, :]
        same = narrow_row[:, None] == wide_row[None, :]
    else:
        step = rate[:, None] * place[None, :] + phase[:, None]
        same = wide_row[:, None] == narrow_row[None, :]
    return split(jnp.where(same, cosine(step, 2 * devices) * scale, 0.0))


def local_table(position, devices, rows, block, transpose):
    length = 2 * devices * rows
    stride = 2 * devices
    fine = block // RADIX
    quart = rows // RADIX
    first = position == 0
    out = jnp.arange(4 * quart, dtype=jnp.int32)
    group, out_part, order = out // (2 * quart), out // quart % 2, out % quart
    rate = jnp.where(first, stride * order + group * devices, stride * (order + 2 * quart * group) + position)
    inp = jnp.arange(2 * devices * fine, dtype=jnp.int32)
    in_part = inp // fine % 2
    base = inp // (2 * fine) * block + inp % fine * RADIX
    in_phase = jnp.where(first, 0, in_part)
    side = jnp.where(first, group, 2)
    digit = jnp.arange(RADIX, dtype=jnp.int32)[:, None, None]
    quarter = length // 4
    if transpose:
        row = digit + base[None, :, None]
        step = row * rate[None, None, :] + quarter * (out_part[None, None, :] - in_phase[None, :, None])
        keep = (side[None, :] == 2) | (side[None, :] == in_part[:, None])
    else:
        row = digit + base[None, None, :]
        step = row * rate[None, :, None] + quarter * (out_part[None, :, None] - in_phase[None, None, :])
        keep = (side[:, None] == 2) | (side[:, None] == in_part[None, :])
    return split(jnp.where(keep[None], cosine(step, length), 0.0))


def filter_tables(position, member, members, rows):
    first = position == 0
    half = rows // 2
    out = jnp.arange(rows + 8, dtype=jnp.int32)
    order = jnp.minimum(out, rows - 1)
    upper = order >= half
    here = jnp.where(first, jnp.where(upper, rows + order - half, order), order)
    there = jnp.where(
        first,
        jnp.where(upper, 2 * rows - 1 - (order - half), (rows - order) % rows),
        2 * rows - 1 - order,
    )
    stored = jnp.arange(2 * rows, dtype=jnp.int32)
    part = 2 * rows // members
    stored = (member + members - stored // part) % members * part + stored % part
    hit_here = (stored[None, :] == here[:, None]).astype(jnp.float32)
    hit_there = (stored[None, :] == there[:, None]).astype(jnp.float32)
    weight = jnp.where(first & (order == 0), 0.25, 0.5)[:, None]
    even = weight * (hit_here + hit_there)
    odd = weight * (hit_here - hit_there)
    edge = jnp.where(first & (out[:, None] == rows) & (stored[None, :] == half), 0.5, 0.0)
    even = jnp.where((out < rows)[:, None], even, edge)
    return even.astype(jnp.bfloat16), odd[:rows].astype(jnp.bfloat16)


def dot(high, low, x):
    return jnp.dot(
        jnp.concatenate([high, low], axis=1),
        jnp.concatenate([x, x], axis=0),
        preferred_element_type=jnp.float32,
    )


def each_block(width, step):
    def go(i, carry):
        step(pl.ds(pl.multiple_of(i * LANES, LANES), LANES))
        return carry

    lax.fori_loop(0, width // LANES, go, 0)


def cross_kernel(high_ref, low_ref, x_ref, o_ref):
    def step(cols):
        o_ref[:, cols] = dot(high_ref[...], low_ref[...], x_ref[:, cols]).astype(o_ref.dtype)

    each_block(x_ref.shape[1], step)


def filter_kernel(even_ref, odd_ref, *refs):
    *pieces, even_out, odd_out = refs
    rows = pieces[0].shape[1]
    even = odd = 0.0
    for shift, piece in enumerate(pieces):
        cols = slice(shift * rows, (shift + 1) * rows)
        even += jnp.dot(even_ref[:, cols], piece[0], preferred_element_type=jnp.float32)
        odd += jnp.dot(odd_ref[:, cols], piece[1], preferred_element_type=jnp.float32)
    even_out[...] = even
    odd_out[...] = odd


def local_kernel(mh_ref, ml_ref, gh_ref, gl_ref, even_ref, odd_ref, x_ref, o_ref):
    rows = odd_ref.shape[0]
    quart = rows // RADIX

    def step(cols):
        v = []
        for digit in range(RADIX):
            x = x_ref[:, digit, :, cols]
            v.append(dot(mh_ref[digit], ml_ref[digit], x.reshape(-1, x.shape[-1])))
        sum02, sum13, gap02, gap13 = v[0] + v[2], v[1] + v[3], v[0] - v[2], v[1] - v[3]
        edge = (sum02[:8] - sum13[:8]) * even_ref[rows:, cols]
        total = sum02 + sum13
        packed = [[] for _ in range(RADIX)]
        for group in range(2):
            at = 2 * group * quart
            re, im = slice(at, at + quart), slice(at + quart, at + 2 * quart)
            parts = []
            for turn, (real, imag) in enumerate(
                ((total[re], total[im]), (gap02[re] + gap13[im], gap02[im] - gap13[re]))
            ):
                here = pl.ds(at + turn * quart, quart)
                even, odd = even_ref[here, cols], odd_ref[here, cols]
                parts.append((real * even - imag * odd, real * odd + imag * even))
            (r0, i0), (r1, i1) = parts
            for digit, (real, imag) in enumerate(
                ((r0 + r1, i0 + i1), (r0 - i1, i0 + r1), (r0 - r1, i0 - i1), (r0 + i1, i0 - r1))
            ):
                if group == 0:
                    top = real[:8] + edge if digit % 2 == 0 else real[:8] - edge
                    packed[digit].append(jnp.concatenate([top, real[8:]], axis=0))
                else:
                    packed[digit].append(real)
                packed[digit].append(imag)
        for digit in range(RADIX):
            b = jnp.concatenate(packed[digit], axis=0).astype(jnp.bfloat16)
            y = dot(gh_ref[digit], gl_ref[digit], b)
            o_ref[:, digit, :, cols] = y.reshape(o_ref.shape[0], o_ref.shape[2], -1).astype(o_ref.dtype)

    each_block(odd_ref.shape[1], step)


def call(kernel, operands, outs, grant):
    vmem = pl.BlockSpec(memory_space=pltpu.VMEM)
    return pl.pallas_call(
        kernel,
        in_specs=[vmem] * len(operands),
        out_specs=vmem,
        out_shape=outs,
        compiler_params=pltpu.CompilerParams(vmem_limit_bytes=grant << 20),
    )(*operands)


def exchange(array):
    return lax.all_to_all(array, "ctx", split_axis=0, concat_axis=0, tiled=True)


def body(gate_in, values, gate_out, bias, spectrum):
    devices = lax.axis_size("ctx")
    members = lax.axis_size("fsdp")
    rows, channels = gate_in.shape
    block = rows // devices
    length = 2 * rows * devices
    position = lax.axis_index("ctx")
    member = lax.axis_index("fsdp")
    shape = jax.ShapeDtypeStruct

    mixed = (gate_in.astype(jnp.float32) * values.astype(jnp.float32)).astype(jnp.bfloat16)
    mixed = lax.optimization_barrier(mixed)
    stage = exchange(mixed.reshape(devices, block, channels))

    held = []
    for shift in range(members):
        target = lax.rem(member + shift, members)
        piece = lax.dynamic_slice_in_dim(spectrum, target * channels, channels, 2)
        if shift > 0:
            ring = [(m, (m + shift) % members) for m in range(members)]
            piece = lax.ppermute(piece, "fsdp", ring)
        held.append(piece)

    cross = cross_table(devices, block, False, 1.0)
    cross_back = cross_table(devices, block, True, 2.0 / length)
    local = local_table(position, devices, rows, block, False)
    local_back = local_table(position, devices, rows, block, True)
    even, odd = filters(filter_tables(position, member, members, rows), held, rows, channels)

    spread = call(cross_kernel, (*cross, stage.reshape(rows, channels)), shape((2 * rows, channels), jnp.bfloat16), 12)
    stage = exchange(spread.reshape(devices, 2 * block, channels))
    wide = (devices, RADIX, 2 * block // RADIX, channels)
    turned = call(local_kernel, (*local, *local_back, even, odd, stage.reshape(wide)), shape(wide, jnp.bfloat16), 24)
    stage = exchange(turned.reshape(devices, 2 * block, channels))
    folded = call(
        cross_kernel, (*cross_back, stage.reshape(2 * rows, channels)), shape((rows, channels), jnp.bfloat16), 12
    )
    restored = exchange(folded.reshape(devices, block, channels)).reshape(rows, channels)
    convolved = restored.astype(jnp.float32) + bias[None, :] * mixed.astype(jnp.float32)
    return (gate_out.astype(jnp.float32) * convolved).astype(jnp.bfloat16)


def filters(tables, held, rows, channels):
    def whole(array):
        return pl.BlockSpec(array.shape, lambda i: (0, 0))

    def columns(*dims):
        return pl.BlockSpec((*dims, LANES), lambda i: (0,) * len(dims) + (i,))

    return pl.pallas_call(
        filter_kernel,
        grid=(channels // LANES,),
        in_specs=[whole(t) for t in tables] + [columns(*h.shape[:-1]) for h in held],
        out_specs=(columns(rows + 8), columns(rows)),
        out_shape=(
            jax.ShapeDtypeStruct((rows + 8, channels), jnp.float32),
            jax.ShapeDtypeStruct((rows, channels), jnp.float32),
        ),
        name="filters",
        compiler_params=pltpu.CompilerParams(vmem_limit_bytes=16 << 20),
    )(*tables, *held)


def solution(mesh):
    return jax.shard_map(
        body,
        mesh=mesh,
        in_specs=(
            P("ctx", "fsdp"),
            P("ctx", "fsdp"),
            P("ctx", "fsdp"),
            P("fsdp"),
            P(None, ("ctx", "fsdp"), None),
        ),
        out_specs=P("ctx", "fsdp"),
        check_vma=False,
    )
```

time: 167 us -> 153 us (0.916)
  Pallas kernels: 41.6 us -> 18.2 us
  local copies, waits for them, and re-layouts: 7.05 us -> 20.2 us
  other arithmetic: 30.5 us -> 21.5 us
  waiting for transfers between devices: 40.4 us -> 47.7 us
    pallas_call x4, Pallas kernels: 41.6 us -> 18.2 us  [the longest x3 13.4 us: call(): pl.pallas_call(kernel, in_specs=[vmem] * len(operands), out_specs=vmem, o...]
    unnamed x14 -> x38, local copies, waits for them, and re-layouts: 2.3 us -> 15.3 us
    all_to_all x3, waiting for transfers between devices: 40.4 us -> 47.7 us  [exchange(): return lax.all_to_all(array, 'ctx', split_axis=0, concat_axis=0, tiled=True)]
    convert_element_type x3 -> x4, other arithmetic: 19.9 us -> 13.1 us  [split(): return (high.astype(jnp.bfloat16), (table - high).astype(jnp.bfloat16))]
    another operation x1, other arithmetic: 2.9 us -> 0.29 us
    mul x1 -> x2, other arithmetic: 0.02 us -> 1.85 us  [the longest x1 0.93 us: local_table(): quarter * (out_part[None, :, None] - in_phase[None, None, :])]
  transfers between devices with their start and end apart: 6 -> 6, of which waited for: 3 -> 3; matrix products, arithmetic and copies ran while one was open for 17% -> 12% of each run, Pallas kernels for 8% -> 6%
where the time goes in v2:
time: 153 us; the launch traced here: 152 us
  waiting for transfers between devices  47.7 us (31%)
  starting transfers between devices  23.7 us (15%)
  other arithmetic  21.5 us (14%)
  blocking collectives  20.6 us (13%)
  local copies, waits for them, and re-layouts  20.2 us (13%)
  Pallas kernels  18.2 us (12%)
    all_to_all x3, waiting for transfers between devices, exchange(): return lax.all_to_all(array, 'ctx', split_axis=0, concat_axis=0, tiled=True)  47.7 us
    all_to_all x1, blocking collectives, exchange(): return lax.all_to_all(array, 'ctx', split_axis=0, concat_axis=0, tiled=True)  20.6 us
    all_to_all x3, starting transfers between devices, exchange(): return lax.all_to_all(array, 'ctx', split_axis=0, concat_axis=0, tiled=True)  18 us
    unnamed x38, local copies, waits for them, and re-layouts  15.3 us
    pallas_call x3, Pallas kernels, call(): pl.pallas_call(kernel, in_specs=[vmem] * len(operands), out_specs=vmem, o...  13.4 us
    convert_element_type x4, other arithmetic, split(): return (high.astype(jnp.bfloat16), (table - high).astype(jnp.bfloat16))  13.1 us
    ppermute x3, starting transfers between devices, body(): piece = lax.ppermute(piece, 'fsdp', ring)  5.63 us
    pallas_call x1, Pallas kernels, filters(): pl.pallas_call(filter_kernel, grid=(channels // LANES,), in_specs=[whole(...  4.84 us
  transfers between devices with their start and end apart: 6, of which 3 were waited for; matrix products, arithmetic and copies ran while one was open for 12% of the time, Pallas kernels for 6%

profile of v2, /device:TPU:1, one launch (start us, length us, event | category | flops | bytes accessed | tf_op | source)
XLA Modules:
  0.0 152.2 jit_solution(11987580631467684511)
XLA Ops:
  0.0 0.0 copy-start.14
  0.0 0.0 copy-start.15
  0.0 4.6 %constant_dynamic-slice_fusion = (bf16[2,256,1024]{2,1,0:T(8,128)(2,1)}, bf16[2,256,1024]{2,1,0:T(8,128)(2,1)}, bf16[2,256,1024]{2,1,0:T(8,128)(2,1)}, bf16[2,256,1024]{2,1,0:T(8,128)(2,1)}) fusion(bf16[2,256,4096]{2,1,0:T(8,128)(2,1)} %param.9, s32[]{:T(128)S(6)} %select_n.597, s32[]{:T(128)S(6)} %select_n.595, s32[]{:T(128)S(6)} %select_n.594, ...), kind=kLoop, calls=%fused_computation.178 | loop fusion | bytes 8388624 | tf_op jit(solution)/shard_map/dynamic_slice | solution.py:214
  4.6 2.0 %collective-permute-start = (bf16[2,256,1024]{2,1,0:T(8,128)(2,1)}, bf16[2,256,1024]{2,1,0:T(8,128)(2,1)}, u32[]{:S(2)}, u32[]{:S(2)}) collective-permute-start(bf16[2,256,1024]{2,1,0:T(8,128)(2,1)} %get-tuple-element.10), channel_id=1, source_target_pairs={{0,1},{1,2},{2,3},{3,0},{4,5},{5,6},{6,7},{7,4},{8,9},{9,10},{10,1... | collective-permute-start | bytes 3145736 | tf_op jit(solution)/shard_map/ppermute | solution.py:217
  6.7 2.5 %collective-permute-start.1 = (bf16[2,256,1024]{2,1,0:T(8,128)(2,1)}, bf16[2,256,1024]{2,1,0:T(8,128)(2,1)}, u32[]{:S(2)}, u32[]{:S(2)}) collective-permute-start(bf16[2,256,1024]{2,1,0:T(8,128)(2,1)} %get-tuple-element.12), channel_id=1, source_target_pairs={{0,2},{1,3},{2,0},{3,1},{4,6},{5,7},{6,4},{7,5},{8,10},{9,11},{10,... | collective-permute-start | bytes 3145736 | tf_op jit(solution)/shard_map/ppermute | solution.py:217
  9.1 1.2 collective-permute-start.2
  10.3 0.0 copy-done.14
  10.3 0.0 copy-done.15
  10.3 1.4 multiply_convert_fusion
  11.6 9.6 %all-to-all-start = ((bf16[32,16,1024]{2,1,0:T(8,128)(2,1)}), bf16[32,16,1024]{2,1,0:T(8,128)(2,1)S(1)}, u32[]{:S(2)}, u32[]{:S(2)}) async-start(bf16[32,16,1024]{2,1,0:T(8,128)(2,1)} %bitcast), calls=%async_computation | async-start | bytes 2097152 | tf_op jit(solution)/shard_map/all_to_all | solution.py:194
  21.3 0.0 copy-start.17
  21.4 0.9 subtract_multiply_fusion
  22.4 0.2 compare_or_fusion
  22.5 0.9 subtract_multiply_fusion.1
  23.5 1.2 select_convert_fusion.even_ref
  24.7 3.3 %fusion.3 = (bf16[1024,512]{1,0:T(8,128)(2,1)S(1)}, bf16[1024,512]{1,0:T(8,128)(2,1)}) fusion(s32[1024]{0:T(1024)S(1)} %get-tuple-element.23, s32[512]{0:T(512)S(1)} %get-tuple-element.25, s32[1024]{0:T(1024)S(1)} %get-tuple-element.24, s32[512]{0:T(512)S(1)} %get-tuple-element.26, s32[1024]{0:T(1024)S(1)} %fusion.35), kind=kLoop, calls=%fused_computation.14 | loop fusion | flops 15204352 | bytes 2113536 | tf_op jit(solution)/shard_map/convert_element_type | solution.py:28
  28.0 0.0 copy-done.17
  28.0 10.2 %all-to-all-done = bf16[32,16,1024]{2,1,0:T(8,128)(2,1)S(1)} async-done(((bf16[32,16,1024]{2,1,0:T(8,128)(2,1)}), bf16[32,16,1024]{2,1,0:T(8,128)(2,1)S(1)}, u32[]{:S(2)}, u32[]{:S(2)}) %all-to-all-start) | async-done | bytes 1048608 | tf_op jit(solution)/shard_map/all_to_all | solution.py:194
  38.2 0.0 copy-start.6
  38.2 1.2 copy-done.6
  39.4 4.2 %shard_map.55 = bf16[1024,1024]{1,0:T(8,128)(2,1)} custom-call(bf16[1024,512]{1,0:T(8,128)(2,1)S(1)} %copy-done.6, bf16[1024,512]{1,0:T(8,128)(2,1)S(1)} %get-tuple-element.17.low_ref, bf16[512,1024]{1,0:T(8,128)(2,1)S(1)} %bitcast.13), custom_call_target="tpu_custom_call" | custom-call | tf_op jit(solution)/shard_map/pallas_call | solution.py:184
  43.6 3.9 %all-to-all-start.1 = ((bf16[32,32,1024]{2,1,0:T(8,128)(2,1)}), bf16[32,32,1024]{2,1,0:T(8,128)(2,1)S(1)}, u32[]{:S(2)}, u32[]{:S(2)}) async-start(bf16[32,32,1024]{2,1,0:T(8,128)(2,1)} %bitcast.2), calls=%async_computation.1 | async-start | bytes 4194304 | tf_op jit(solution)/shard_map/all_to_all | solution.py:194
  47.6 0.2 compare_or_fusion.1
  47.8 0.0 slice-start
  47.8 0.3 compare_convert_fusion.1
  48.1 0.3 slice-done
  48.4 0.0 copy-start.13
  48.4 0.3 fusion.5.odd_ref
  48.7 0.0 copy-start.12
  48.7 0.7 copy-done.13
  49.4 0.0 copy-start.7
  49.4 3.3 %fusion.1 = (bf16[4,512,256]{2,1,0:T(8,128)(2,1)}, bf16[4,512,256]{2,1,0:T(8,128)(2,1)}) fusion(s32[512,256]{1,0:T(8,128)S(1)} %copy-done.13, s32[512]{0:T(512)S(1)} %get-tuple-element.32, s32[4,256]{1,0:T(4,128)S(1)} %iota_add_fusion, pred[512,256]{1,0:T(8,128)(4,1)S(1)} %compare_or_fusion.1), kind=kLoop, calls=%fused_computation.12 | loop fusion | flops 14680064 | bytes 2758656 | tf_op jit(solution)/shard_map/convert_element_type | solution.py:28
  52.7 0.0 copy-done.12
  52.7 3.1 %fusion.2 = (bf16[4,256,512]{2,1,0:T(8,128)(2,1)}, bf16[4,256,512]{2,1,0:T(8,128)(2,1)}) fusion(s32[256,512]{1,0:T(8,128)S(1)} %copy-done.12, s32[512]{0:T(512)S(1)} %get-tuple-element.32, s32[4,256]{1,0:T(4,128)S(1)} %iota_add_fusion, pred[256,512]{1,0:T(8,128)(4,1)S(1)} %compare_or_fusion), kind=kLoop, calls=%fused_computation.13 | loop fusion | flops 14680064 | bytes 2758656 | tf_op jit(solution)/shard_map/convert_element_type | solution.py:28
  55.9 0.0 collective-permute-done.refs_1_
  55.9 0.0 collective-permute-done.1.refs_2_
  55.9 0.0 collective-permute-done.2.refs_3_
  55.9 0.0 copy-done.7
  55.9 4.8 %filters.1 = (f32[520,1024]{1,0:T(8,128)S(1)}, f32[512,1024]{1,0:T(8,128)S(1)}) custom-call(bf16[520,1024]{1,0:T(8,128)(2,1)S(1)} %select_convert_fusion.even_ref, bf16[512,1024]{1,0:T(8,128)(2,1)S(1)} %fusion.5.odd_ref, bf16[2,256,1024]{2,1,0:T(8,128)(2,1)S(1)} %copy-done.7, bf16[2,256,1024]{2,1,0:T(8,128)(2,1)} %collective-permute-done.refs_1_, ...), custom_call_target="tpu_custom_call" | custom-call | tf_op jit(solution)/shard_map/filters/pallas_call | solution.py:246
  60.7 0.0 copy-start.8
  60.7 1.4 copy-done.8
  62.1 0.0 copy-start.10
  62.1 1.3 copy-done.10
  63.4 12.5 %all-to-all-done.1 = bf16[32,32,1024]{2,1,0:T(8,128)(2,1)S(1)} async-done(((bf16[32,32,1024]{2,1,0:T(8,128)(2,1)}), bf16[32,32,1024]{2,1,0:T(8,128)(2,1)S(1)}, u32[]{:S(2)}, u32[]{:S(2)}) %all-to-all-start.1) | async-done | bytes 2097184 | tf_op jit(solution)/shard_map/all_to_all | solution.py:194
  75.9 1.2 copy-done.1
  77.1 1.2 copy-done.2
  78.4 1.2 copy-done.3
  79.6 1.2 copy-done.4
  80.8 1.6 %copy-done.9 = f32[520,1024]{1,0:T(8,128)S(1)} copy-done((f32[520,1024]{1,0:T(8,128)S(1)}, f32[520,1024]{1,0:T(8,128)}, u32[]{:S(2)}) %copy-start.9) | copy-done | bytes 2129944
  82.4 1.6 %copy-done.11 = f32[512,1024]{1,0:T(8,128)S(1)} copy-done((f32[512,1024]{1,0:T(8,128)S(1)}, f32[512,1024]{1,0:T(8,128)}, u32[]{:S(2)}) %copy-start.11) | copy-done | bytes 2097176
  84.0 6.3 %shard_map.56 = bf16[32,4,8,1024]{3,2,1,0:T(8,128)(2,1)S(1)} custom-call(bf16[4,512,256]{2,1,0:T(8,128)(2,1)S(1)} %copy-done.2, bf16[4,512,256]{2,1,0:T(8,128)(2,1)S(1)} %copy-done.1, bf16[4,256,512]{2,1,0:T(8,128)(2,1)S(1)} %copy-done.4, bf16[4,256,512]{2,1,0:T(8,128)(2,1)S(1)} %copy-done.3, f32[520,1024]{1,0:T(8,128)S(1)} %copy-done.9, ...), custom_call_target="tpu_custom_call" | custom-call | tf_op jit(solution)/shard_map/pallas_call | solution.py:184
  90.3 0.0 copy-start
  90.3 1.4 copy-done
  91.7 4.5 %all-to-all-start.2 = ((bf16[32,32,1024]{2,1,0:T(8,128)(2,1)}), bf16[32,32,1024]{2,1,0:T(8,128)(2,1)S(1)}, u32[]{:S(2)}, u32[]{:S(2)}) async-start(bf16[32,32,1024]{2,1,0:T(8,128)(2,1)} %bitcast.12), calls=%async_computation.2 | async-start | bytes 4194304 | tf_op jit(solution)/shard_map/all_to_all | solution.py:194
  96.2 3.4 %fusion = (bf16[512,1024]{1,0:T(8,128)(2,1)S(1)}, bf16[512,1024]{1,0:T(8,128)(2,1)}) fusion(s32[1024]{0:T(1024)S(1)} %get-tuple-element.23, s32[1024]{0:T(1024)S(1)} %get-tuple-element.24, s32[512]{0:T(512)S(1)} %get-tuple-element.25, s32[1024]{0:T(1024)S(1)} %fusion.35, s32[512]{0:T(512)S(1)} %get-tuple-element.26), kind=kLoop, calls=%fused_computation.11 | loop fusion | flops 15728640 | bytes 2113536 | tf_op jit(solution)/shard_map/convert_element_type | solution.py:28
  99.6 25.0 %all-to-all-done.2 = bf16[32,32,1024]{2,1,0:T(8,128)(2,1)S(1)} async-done(((bf16[32,32,1024]{2,1,0:T(8,128)(2,1)}), bf16[32,32,1024]{2,1,0:T(8,128)(2,1)S(1)}, u32[]{:S(2)}, u32[]{:S(2)}) %all-to-all-start.2) | async-done | bytes 2097184 | tf_op jit(solution)/shard_map/all_to_all | solution.py:194
  124.6 1.2 copy-done.5
  125.8 2.9 %shard_map.57 = bf16[512,1024]{1,0:T(8,128)(2,1)S(1)} custom-call(bf16[512,1024]{1,0:T(8,128)(2,1)S(1)} %copy-done.5, bf16[512,1024]{1,0:T(8,128)(2,1)S(1)} %get-tuple-element.19.low_ref, bf16[1024,1024]{1,0:T(8,128)(2,1)S(1)} %bitcast.10), custom_call_target="tpu_custom_call" | custom-call | tf_op jit(solution)/shard_map/pallas_call | solution.py:184
  128.7 0.0 copy-start.16
  128.7 0.0 copy-start.18
  128.7 20.6 %all_to_all.20 = bf16[32,16,1024]{2,1,0:T(8,128)(2,1)S(1)} all-to-all(bf16[32,16,1024]{2,1,0:T(8,128)(2,1)S(1)} %bitcast.14), channel_id=1, replica_groups=mesh['ctx'=32,'fsdp'=4] {'ctx'}, dimensions={0} | all-to-all | bytes 2097152 | tf_op jit(solution)/shard_map/all_to_all | solution.py:194
  149.4 0.0 copy-done.16
  149.4 0.0 copy-done.18
  149.4 2.9 %fusion.7 = bf16[512,1024]{1,0:T(8,128)(2,1)} fusion(bf16[512,1024]{1,0:T(8,128)(2,1)} %multiply_convert_fusion, bf16[512,1024]{1,0:T(8,128)(2,1)S(1)} %copy-done.16, bf16[32,16,1024]{2,1,0:T(8,128)(2,1)S(1)} %all_to_all.20, f32[1024]{0:T(1024)S(1)} %copy-done.18), kind=kLoop, calls=%fused_computation.20 | loop fusion | flops 3670016 | bytes 4198400 | tf_op jit(solution)/shard_map/convert_element_type | solution.py:236
  (21 shorter events, 0.1 us)
Async XLA Ops:
  0.0 10.3 %copy-start.14 = (bf16[512,1024]{1,0:T(8,128)(2,1)S(1)}, bf16[512,1024]{1,0:T(8,128)(2,1)}, u32[]{:S(2)}) copy-start(bf16[512,1024]{1,0:T(8,128)(2,1)} %param.6) | copy-start | bytes 3145732
  0.0 10.3 %copy-start.15 = (bf16[512,1024]{1,0:T(8,128)(2,1)S(1)}, bf16[512,1024]{1,0:T(8,128)(2,1)}, u32[]{:S(2)}) copy-start(bf16[512,1024]{1,0:T(8,128)(2,1)} %param.5) | copy-start | bytes 3145732
  4.6 51.2 %collective-permute-start = (bf16[2,256,1024]{2,1,0:T(8,128)(2,1)}, bf16[2,256,1024]{2,1,0:T(8,128)(2,1)}, u32[]{:S(2)}, u32[]{:S(2)}) collective-permute-start(bf16[2,256,1024]{2,1,0:T(8,128)(2,1)} %get-tuple-element.10), channel_id=1, source_target_pairs={{0,1},{1,2},{2,3},{3,0},{4,5},{5,6},{6,7},{7,4},{8,9},{9,10},{10,1... | collective-permute-start | bytes 3145736 | tf_op jit(solution)/shard_map/ppermute | solution.py:217
  6.7 49.2 %collective-permute-start.1 = (bf16[2,256,1024]{2,1,0:T(8,128)(2,1)}, bf16[2,256,1024]{2,1,0:T(8,128)(2,1)}, u32[]{:S(2)}, u32[]{:S(2)}) collective-permute-start(bf16[2,256,1024]{2,1,0:T(8,128)(2,1)} %get-tuple-element.12), channel_id=1, source_target_pairs={{0,2},{1,3},{2,0},{3,1},{4,6},{5,7},{6,4},{7,5},{8,10},{9,11},{10,... | collective-permute-start | bytes 3145736 | tf_op jit(solution)/shard_map/ppermute | solution.py:217
  9.1 46.8 %collective-permute-start.2 = (bf16[2,256,1024]{2,1,0:T(8,128)(2,1)}, bf16[2,256,1024]{2,1,0:T(8,128)(2,1)}, u32[]{:S(2)}, u32[]{:S(2)}) collective-permute-start(bf16[2,256,1024]{2,1,0:T(8,128)(2,1)} %get-tuple-element.9), channel_id=1, source_target_pairs={{0,3},{1,0},{2,1},{3,2},{4,7},{5,4},{6,5},{7,6},{8,11},{9,8},{10,9... | collective-permute-start | bytes 3145736 | tf_op jit(solution)/shard_map/ppermute | solution.py:217
  11.6 26.5 %all-to-all-start = ((bf16[32,16,1024]{2,1,0:T(8,128)(2,1)}), bf16[32,16,1024]{2,1,0:T(8,128)(2,1)S(1)}, u32[]{:S(2)}, u32[]{:S(2)}) async-start(bf16[32,16,1024]{2,1,0:T(8,128)(2,1)} %bitcast), calls=%async_computation | async-start | bytes 2097152 | tf_op jit(solution)/shard_map/all_to_all | solution.py:194
  21.3 6.7 %copy-start.17 = (f32[520]{0:T(1024)}, f32[520]{0:T(1024)S(1)}, u32[]{:S(2)}) copy-start(f32[520]{0:T(1024)S(1)} %fusion.52) | copy-start | bytes 6244
  38.2 1.2 copy-start.6
  43.6 32.3 %all-to-all-start.1 = ((bf16[32,32,1024]{2,1,0:T(8,128)(2,1)}), bf16[32,32,1024]{2,1,0:T(8,128)(2,1)S(1)}, u32[]{:S(2)}, u32[]{:S(2)}) async-start(bf16[32,32,1024]{2,1,0:T(8,128)(2,1)} %bitcast.2), calls=%async_computation.1 | async-start | bytes 4194304 | tf_op jit(solution)/shard_map/all_to_all | solution.py:194
  47.8 0.6 slice-start
  48.4 1.0 copy-start.13
  48.7 4.0 %copy-start.12 = (s32[256,512]{1,0:T(8,128)S(1)}, s32[256,512]{1,0:T(8,128)}, u32[]{:S(2)}) copy-start(s32[256,512]{1,0:T(8,128)} %subtract_multiply_fusion) | copy-start | bytes 1572868
  49.4 6.4 %copy-start.7 = (bf16[2,256,1024]{2,1,0:T(8,128)(2,1)S(1)}, bf16[2,256,1024]{2,1,0:T(8,128)(2,1)}, u32[]{:S(2)}) copy-start(bf16[2,256,1024]{2,1,0:T(8,128)(2,1)} %get-tuple-element.11.refs_0_) | copy-start | bytes 3145732
  60.7 1.4 copy-start.8
  62.1 1.3 copy-start.10
  75.9 1.2 copy-start.1
  77.1 1.2 copy-start.2
  78.3 1.2 copy-start.3
  79.6 1.2 copy-start.4
  80.8 1.6 %copy-start.9 = (f32[520,1024]{1,0:T(8,128)S(1)}, f32[520,1024]{1,0:T(8,128)}, u32[]{:S(2)}) copy-start(f32[520,1024]{1,0:T(8,128)} %copy-done.8) | copy-start | bytes 6389764
  82.4 1.6 %copy-start.11 = (f32[512,1024]{1,0:T(8,128)S(1)}, f32[512,1024]{1,0:T(8,128)}, u32[]{:S(2)}) copy-start(f32[512,1024]{1,0:T(8,128)} %copy-done.10) | copy-start | bytes 6291460
  90.3 1.4 copy-start
  91.7 32.9 %all-to-all-start.2 = ((bf16[32,32,1024]{2,1,0:T(8,128)(2,1)}), bf16[32,32,1024]{2,1,0:T(8,128)(2,1)S(1)}, u32[]{:S(2)}, u32[]{:S(2)}) async-start(bf16[32,32,1024]{2,1,0:T(8,128)(2,1)} %bitcast.12), calls=%async_computation.2 | async-start | bytes 4194304 | tf_op jit(solution)/shard_map/all_to_all | solution.py:194
  124.6 1.2 copy-start.5
  128.7 20.7 %copy-start.16 = (bf16[512,1024]{1,0:T(8,128)(2,1)S(1)}, bf16[512,1024]{1,0:T(8,128)(2,1)}, u32[]{:S(2)}) copy-start(bf16[512,1024]{1,0:T(8,128)(2,1)} %param.7) | copy-start | bytes 3145732
  128.7 20.7 %copy-start.18 = (f32[1024]{0:T(1024)S(1)}, f32[1024]{0:T(1024)}, u32[]{:S(2)}) copy-start(f32[1024]{0:T(1024)} %param.8) | copy-start | bytes 12292

commit v3 on v2

--- a/solution.py
+++ b/solution.py
@@ -1,3 +1,4 @@
+import functools
 import math
 
 import jax
@@ -10,6 +11,7 @@
 
 LANES = 256
 RADIX = 4
+SPREAD = 1.624475
 
 
 def cosine(step, modulus):
@@ -33,7 +35,7 @@
     return index % fine * RADIX + index // (2 * fine) % RADIX, index // fine % 2
 
 
-def cross_table(devices, block, transpose, scale):
+def cross_table(devices, block, transpose):
     wide = jnp.arange(2 * devices * block, dtype=jnp.int32)
     residue = wide // (2 * block)
     wide_row, part = message(wide, block)
@@ -48,7 +50,7 @@
     else:
         step = rate[:, None] * place[None, :] + phase[:, None]
         same = wide_row[:, None] == narrow_row[None, :]
-    return split(jnp.where(same, cosine(step, 2 * devices) * scale, 0.0))
+    return jnp.where(same, cosine(step, 2 * devices) * SPREAD, 0.0).astype(jnp.bfloat16)
 
 
 def local_table(position, devices, rows, block, transpose):
@@ -113,15 +115,29 @@
 
 def each_block(width, step):
     def go(i, carry):
-        step(pl.ds(pl.multiple_of(i * LANES, LANES), LANES))
+        step(i, pl.ds(pl.multiple_of(i * LANES, LANES), LANES))
         return carry
 
     lax.fori_loop(0, width // LANES, go, 0)
 
 
-def cross_kernel(high_ref, low_ref, x_ref, o_ref):
-    def step(cols):
-        o_ref[:, cols] = dot(high_ref[...], low_ref[...], x_ref[:, cols]).astype(o_ref.dtype)
+def cross_kernel(scale, table_ref, x_ref, o_hbm, o_buf, o_sem):
+    def store(i, cols):
+        return pltpu.make_async_copy(o_buf.at[:, cols], o_hbm.at[:, cols], o_sem.at[i])
+
+    def step(i, cols):
+        acc = jnp.dot(table_ref[...], x_ref[:, cols], preferred_element_type=jnp.float32)
+        o_buf[:, cols] = (acc * scale).astype(o_buf.dtype)
+        store(i, cols).start()
+
+    each_block(x_ref.shape[1], step)
+    each_block(x_ref.shape[1], lambda i, cols: store(i, cols).wait())
+
+
+def fold_kernel(scale, table_ref, x_ref, o_ref):
+    def step(i, cols):
+        acc = jnp.dot(table_ref[...], x_ref[:, cols], preferred_element_type=jnp.float32)
+        o_ref[:, cols] = (acc * scale).astype(o_ref.dtype)
 
     each_block(x_ref.shape[1], step)
 
@@ -138,15 +154,59 @@
     odd_out[...] = odd
 
 
-def local_kernel(mh_ref, ml_ref, gh_ref, gl_ref, even_ref, odd_ref, x_ref, o_ref):
-    rows = odd_ref.shape[0]
+def local_kernel(
+    mh_hbm, ml_hbm, gh_hbm, gl_hbm, even_hbm, odd_hbm, x_hbm, o_hbm,
+    mh_ref, ml_ref, gh_ref, gl_ref, even_ref, odd_ref, x_ref, o_ref, m_sem, g_sem, h_sem, x_sem, o_sem,
+):
+    rows, width = odd_ref.shape
     quart = rows // RADIX
 
-    def step(cols):
+    def tables(sources, places, sems, digit):
+        return [
+            pltpu.make_async_copy(source.at[digit], place.at[digit], sems.at[n, digit])
+            for n, (source, place) in enumerate(zip(sources, places))
+        ]
+
+    def forward(digit):
+        return tables((mh_hbm, ml_hbm), (mh_ref, ml_ref), m_sem, digit) + [
+            pltpu.make_async_copy(x_hbm.at[:, digit], x_ref.at[:, digit], x_sem.at[digit])
+        ]
+
+    def backward(digit):
+        return tables((gh_hbm, gl_hbm), (gh_ref, gl_ref), g_sem, digit)
+
+    def filters(i, cols):
+        return [
+            pltpu.make_async_copy(even_hbm.at[:, cols], even_ref.at[:, cols], h_sem.at[0, i]),
+            pltpu.make_async_copy(odd_hbm.at[:, cols], odd_ref.at[:, cols], h_sem.at[1, i]),
+        ]
+
+    def store(i, cols):
+        return pltpu.make_async_copy(o_ref.at[:, :, :, cols], o_hbm.at[:, :, :, cols], o_sem.at[i])
+
+    def start(copies):
+        for copy in copies:
+            copy.start()
+
+    def wait(copies):
+        for copy in copies:
+            copy.wait()
+
+    for digit in range(RADIX):
+        start(forward(digit))
+    start(filters(0, pl.ds(0, LANES)))
+    for digit in range(RADIX):
+        start(backward(digit))
+    for i in range(1, width // LANES):
+        start(filters(i, pl.ds(i * LANES, LANES)))
+
+    def step(i, cols):
         v = []
         for digit in range(RADIX):
+            pl.when(i == 0)(lambda digit=digit: wait(forward(digit)))
             x = x_ref[:, digit, :, cols]
             v.append(dot(mh_ref[digit], ml_ref[digit], x.reshape(-1, x.shape[-1])))
+        wait(filters(i, cols))
         sum02, sum13, gap02, gap13 = v[0] + v[2], v[1] + v[3], v[0] - v[2], v[1] - v[3]
         edge = (sum02[:8] - sum13[:8]) * even_ref[rows:, cols]
         total = sum02 + sum13
@@ -172,22 +232,76 @@
                     packed[digit].append(real)
                 packed[digit].append(imag)
         for digit in range(RADIX):
+            pl.when(i == 0)(lambda digit=digit: wait(backward(digit)))
             b = jnp.concatenate(packed[digit], axis=0).astype(jnp.bfloat16)
             y = dot(gh_ref[digit], gl_ref[digit], b)
             o_ref[:, digit, :, cols] = y.reshape(o_ref.shape[0], o_ref.shape[2], -1).astype(o_ref.dtype)
-
-    each_block(odd_ref.shape[1], step)
-
-
-def call(kernel, operands, outs, grant):
+        store(i, cols).start()
+
+    each_block(width, step)
+    each_block(width, lambda i, cols: store(i, cols).wait())
+
+
+def gate_kernel(restored_ref, mixed_ref, gate_ref, bias_ref, o_hbm, o_buf, o_sem):
+    rows = o_buf.shape[0] // o_sem.shape[0]
+    bias = bias_ref[...]
+
+    def store(i):
+        at = pl.ds(i * rows, rows)
+        return pltpu.make_async_copy(o_buf.at[at], o_hbm.at[at], o_sem.at[i])
+
+    for i in range(o_sem.shape[0]):
+        at = slice(i * rows, (i + 1) * rows)
+        convolved = restored_ref[at].astype(jnp.float32) + bias * mixed_ref[at].astype(jnp.float32)
+        o_buf[at] = (gate_ref[at].astype(jnp.float32) * convolved).astype(o_buf.dtype)
+        store(i).start()
+    for i in range(o_sem.shape[0]):
+        store(i).wait()
+
+
+def call(kernel, stored, near, out, scratch, grant):
+    there = pl.BlockSpec(memory_space=pltpu.HBM)
+    return pl.pallas_call(
+        kernel,
+        in_specs=[there] * len(stored) + [pl.BlockSpec(memory_space=pltpu.VMEM)] * len(near),
+        out_specs=there,
+        out_shape=out,
+        scratch_shapes=scratch,
+        compiler_params=pltpu.CompilerParams(vmem_limit_bytes=grant << 20),
+    )(*stored, *near)
+
+
+def apply_cross(table, x, scale):
+    out = jax.ShapeDtypeStruct((table.shape[0], x.shape[1]), jnp.bfloat16)
+    scratch = [pltpu.VMEM(out.shape, out.dtype), pltpu.SemaphoreType.DMA((x.shape[1] // LANES,))]
+    return call(functools.partial(cross_kernel, scale), (), (table, x), out, scratch, 12)
+
+
+def apply_fold(table, x, scale):
     vmem = pl.BlockSpec(memory_space=pltpu.VMEM)
     return pl.pallas_call(
-        kernel,
-        in_specs=[vmem] * len(operands),
+        functools.partial(fold_kernel, scale),
+        in_specs=[vmem] * 2,
         out_specs=vmem,
-        out_shape=outs,
-        compiler_params=pltpu.CompilerParams(vmem_limit_bytes=grant << 20),
-    )(*operands)
+        out_shape=jax.ShapeDtypeStruct((table.shape[0], x.shape[1]), jnp.bfloat16),
+        name="fold",
+        compiler_params=pltpu.CompilerParams(vmem_limit_bytes=12 << 20),
+    )(table, x)
+
+
+def apply_local(tables, even, odd, x):
+    count = x.shape[-1] // LANES
+    dma = pltpu.SemaphoreType.DMA
+    scratch = [pltpu.VMEM(t.shape, t.dtype) for t in (*tables, even, odd, x, x)]
+    scratch += [dma((2, RADIX)), dma((2, RADIX)), dma((2, count)), dma((RADIX,)), dma((count,))]
+    out = jax.ShapeDtypeStruct(x.shape, x.dtype)
+    return call(local_kernel, (*tables, even, odd, x), (), out, scratch, 62)
+
+
+def apply_gate(restored, mixed, gate_out, bias):
+    scratch = [pltpu.VMEM(mixed.shape, mixed.dtype), pltpu.SemaphoreType.DMA((4,))]
+    out = jax.ShapeDtypeStruct(mixed.shape, mixed.dtype)
+    return call(gate_kernel, (), (restored, mixed, gate_out, bias[None, :]), out, scratch, 8)
 
 
 def exchange(array):
@@ -202,38 +316,39 @@
     length = 2 * rows * devices
     position = lax.axis_index("ctx")
     member = lax.axis_index("fsdp")
-    shape = jax.ShapeDtypeStruct
-
+
+    def piece_for(stored, shift):
+        target = lax.rem(member + shift, members)
+        return lax.dynamic_slice_in_dim(stored, target * channels, channels, 2)
+
+    def send(piece, shift):
+        return lax.ppermute(piece, "fsdp", [(m, (m + shift) % members) for m in range(members)])
+
+    far = members // 2
+    held = {}
+    ahead = piece_for(spectrum, far)
+    held[far] = send(ahead, far)
     mixed = (gate_in.astype(jnp.float32) * values.astype(jnp.float32)).astype(jnp.bfloat16)
-    mixed = lax.optimization_barrier(mixed)
+    mixed, later = lax.optimization_barrier((mixed, spectrum))
     stage = exchange(mixed.reshape(devices, block, channels))
-
-    held = []
-    for shift in range(members):
-        target = lax.rem(member + shift, members)
-        piece = lax.dynamic_slice_in_dim(spectrum, target * channels, channels, 2)
-        if shift > 0:
-            ring = [(m, (m + shift) % members) for m in range(members)]
-            piece = lax.ppermute(piece, "fsdp", ring)
-        held.append(piece)
-
-    cross = cross_table(devices, block, False, 1.0)
-    cross_back = cross_table(devices, block, True, 2.0 / length)
+    for shift in (1, members - 1, 0):
+        piece = piece_for(later, shift)
+        held[shift] = send(piece, shift) if shift else piece
+    held = [held[shift] for shift in range(members)]
+
+    cross = cross_table(devices, block, False)
+    cross_back = cross_table(devices, block, True)
     local = local_table(position, devices, rows, block, False)
     local_back = local_table(position, devices, rows, block, True)
     even, odd = filters(filter_tables(position, member, members, rows), held, rows, channels)
 
-    spread = call(cross_kernel, (*cross, stage.reshape(rows, channels)), shape((2 * rows, channels), jnp.bfloat16), 12)
+    spread = apply_cross(cross, stage.reshape(rows, channels), 1.0 / SPREAD)
     stage = exchange(spread.reshape(devices, 2 * block, channels))
-    wide = (devices, RADIX, 2 * block // RADIX, channels)
-    turned = call(local_kernel, (*local, *local_back, even, odd, stage.reshape(wide)), shape(wide, jnp.bfloat16), 24)
+    turned = apply_local(local + local_back, even, odd, stage.reshape(devices, RADIX, -1, channels))
     stage = exchange(turned.reshape(devices, 2 * block, channels))
-    folded = call(
-        cross_kernel, (*cross_back, stage.reshape(2 * rows, channels)), shape((rows, channels), jnp.bfloat16), 12
-    )
+    folded = apply_fold(cross_back, stage.reshape(2 * rows, channels), 2.0 / (length * SPREAD))
     restored = exchange(folded.reshape(devices, block, channels)).reshape(rows, channels)
-    convolved = restored.astype(jnp.float32) + bias[None, :] * mixed.astype(jnp.float32)
-    return (gate_out.astype(jnp.float32) * convolved).astype(jnp.bfloat16)
+    return apply_gate(restored, mixed, gate_out, bias)
 
 
 def filters(tables, held, rows, channels):
@@ -253,7 +368,7 @@
             jax.ShapeDtypeStruct((rows, channels), jnp.float32),
         ),
         name="filters",
-        compiler_params=pltpu.CompilerParams(vmem_limit_bytes=16 << 20),
+        compiler_params=pltpu.CompilerParams(vmem_limit_bytes=62 << 20),
     )(*tables, *held)
 
 

time: 153 us -> 154 us (level)
  Pallas kernels: 18.2 us -> 33.4 us
  local copies, waits for them, and re-layouts: 20.2 us -> 6.22 us
  waiting for transfers between devices: 47.7 us -> 50.8 us
  other arithmetic: 21.5 us -> 18.5 us
    unnamed x38 -> x6, local copies, waits for them, and re-layouts: 15.3 us -> 0.02 us
    pallas_call x3 -> x4, Pallas kernels: 13.4 us -> 26.5 us  [the longest x3 24.7 us: call(): pl.pallas_call(kernel, in_specs=[there] * len(stored) + [pl.BlockSpec(mem...]
    convert_element_type x4 -> x2, other arithmetic: 13.1 us -> 6.44 us  [split(): return (high.astype(jnp.bfloat16), (table - high).astype(jnp.bfloat16))]
    all_to_all x3, waiting for transfers between devices: 47.7 us -> 50.7 us  [exchange(): return lax.all_to_all(array, 'ctx', split_axis=0, concat_axis=0, tiled=True)]
    pallas_call x1, Pallas kernels: 4.84 us -> 6.84 us  [filters(): pl.pallas_call(filter_kernel, grid=(channels // LANES,), in_specs=[whole(...]
    convert_element_type x1 -> x2, other arithmetic: 2.87 us -> 4.8 us  [cross_table(): jnp.where(same, cosine(step, 2 * devices) * SPREAD, 0.0)]
    convert_element_type x1, other arithmetic: 1.37 us -> 2.94 us  [body(): (gate_in.astype(jnp.float32) * values.astype(jnp.float32)).astype(jnp.bfl...]
    dynamic_slice x1 -> x2, local copies, waits for them, and re-layouts: 4.63 us -> 5.88 us  [piece_for(): return lax.dynamic_slice_in_dim(stored, target * channels, channels, 2)]
  transfers between devices with their start and end apart: 6 -> 6, of which waited for: 3 -> 4; matrix products, arithmetic and copies ran while one was open for 12% -> 12% of each run, Pallas kernels for 6% -> 6%
where the time goes in v3:
time: 154 us
  waiting for transfers between devices  50.8 us (33%)
  Pallas kernels  33.4 us (22%)
  starting transfers between devices  23.7 us (15%)
  blocking collectives  20.6 us (13%)
  other arithmetic  18.5 us (12%)
  local copies, waits for them, and re-layouts  6.22 us (4%)
    all_to_all x3, waiting for transfers between devices, exchange(): return lax.all_to_all(array, 'ctx', split_axis=0, concat_axis=0, tiled=True)  50.7 us
    pallas_call x3, Pallas kernels, call(): pl.pallas_call(kernel, in_specs=[there] * len(stored) + [pl.BlockSpec(mem...  24.7 us
    all_to_all x1, blocking collectives, exchange(): return lax.all_to_all(array, 'ctx', split_axis=0, concat_axis=0, tiled=True)  20.6 us
    all_to_all x3, starting transfers between devices, exchange(): return lax.all_to_all(array, 'ctx', split_axis=0, concat_axis=0, tiled=True)  18.7 us
    pallas_call x1, Pallas kernels, filters(): pl.pallas_call(filter_kernel, grid=(channels // LANES,), in_specs=[whole(...  6.84 us
    convert_element_type x2, other arithmetic, split(): return (high.astype(jnp.bfloat16), (table - high).astype(jnp.bfloat16))  6.44 us
    dynamic_slice x2, local copies, waits for them, and re-layouts, piece_for(): return lax.dynamic_slice_in_dim(stored, target * channels, channels, 2)  5.88 us
    ppermute x3, starting transfers between devices, send(): lax.ppermute(piece, 'fsdp', [(m, (m + shift) % members) for m in range(me...  5.02 us
  transfers between devices with their start and end apart: 6, of which 4 were waited for; matrix products, arithmetic and copies ran while one was open for 12% of the time, Pallas kernels for 6%

profile of v3, /device:TPU:1, one launch (start us, length us, event | category | flops | bytes accessed | tf_op | source)
XLA Modules:
  0.0 153.7 jit_solution(15050632359464420222)
XLA Ops:
  0.0 2.9 %multiply_convert_fusion.mixed_ref = bf16[512,1024]{1,0:T(8,128)(2,1)} fusion(bf16[512,1024]{1,0:T(8,128)(2,1)} %param.6, bf16[512,1024]{1,0:T(8,128)(2,1)} %param.5), kind=kLoop, calls=%fused_computation.21 | loop fusion | flops 2097152 | bytes 3145728 | tf_op jit(solution)/shard_map/convert_element_type | solution.py:331
  2.9 3.6 %constant_dynamic-slice_fusion = (bf16[2,256,1024]{2,1,0:T(8,128)(2,1)}, bf16[2,256,1024]{2,1,0:T(8,128)(2,1)}, bf16[2,256,1024]{2,1,0:T(8,128)(2,1)}) fusion(bf16[2,256,4096]{2,1,0:T(8,128)(2,1)} %param.9, s32[]{:T(128)S(6)} %select_n.553, s32[]{:T(128)S(6)} %select_n.551, s32[]{:T(128)S(6)} %select_n.550), kind=kLoop, calls=%fused_computation.169 | loop fusion | bytes 6291468 | tf_op jit(solution)/shard_map/dynamic_slice | solution.py:322
  6.5 2.0 %collective-permute-start = (bf16[2,256,1024]{2,1,0:T(8,128)(2,1)}, bf16[2,256,1024]{2,1,0:T(8,128)(2,1)}, u32[]{:S(2)}, u32[]{:S(2)}) collective-permute-start(bf16[2,256,1024]{2,1,0:T(8,128)(2,1)} %get-tuple-element.14), channel_id=1, source_target_pairs={{0,1},{1,2},{2,3},{3,0},{4,5},{5,6},{6,7},{7,4},{8,9},{9,10},{10,1... | collective-permute-start | bytes 3145736 | tf_op jit(solution)/shard_map/ppermute | solution.py:325
  8.6 1.3 collective-permute-start.2
  9.8 2.3 %constant_dynamic-slice_fusion.1 = bf16[2,256,1024]{2,1,0:T(8,128)(2,1)} fusion(bf16[2,256,4096]{2,1,0:T(8,128)(2,1)} %param.9, s32[]{:T(128)S(6)} %select_n.552), kind=kLoop, calls=%fused_computation.170 | loop fusion | bytes 2097156 | tf_op jit(solution)/shard_map/dynamic_slice | solution.py:322
  12.1 1.7 %collective-permute-start.1 = (bf16[2,256,1024]{2,1,0:T(8,128)(2,1)}, bf16[2,256,1024]{2,1,0:T(8,128)(2,1)}, u32[]{:S(2)}, u32[]{:S(2)}) collective-permute-start(bf16[2,256,1024]{2,1,0:T(8,128)(2,1)} %constant_dynamic-slice_fusion.1), channel_id=1, source_target_pairs={{0,2},{1,3},{2,0},{3,1},{4,6},{5,7},{6,4},{7,5},{8,10},{9,11},{10,... | collective-permute-start | bytes 3145736 | tf_op jit(solution)/shard_map/ppermute | solution.py:325
  13.8 9.6 %all-to-all-start = ((bf16[32,16,1024]{2,1,0:T(8,128)(2,1)}), bf16[32,16,1024]{2,1,0:T(8,128)(2,1)S(1)}, u32[]{:S(2)}, u32[]{:S(2)}) async-start(bf16[32,16,1024]{2,1,0:T(8,128)(2,1)} %bitcast), calls=%async_computation | async-start | bytes 2097152 | tf_op jit(solution)/shard_map/all_to_all | solution.py:308
  23.5 0.0 copy-start.2
  23.6 0.1 subtract_multiply_fusion
  23.7 0.2 compare_or_fusion
  23.9 0.1 subtract_multiply_fusion.1
  24.1 2.1 %select_convert_fusion.even_ref = bf16[520,1024]{1,0:T(8,128)(2,1)} fusion(f32[520]{0:T(1024)S(1)} %fusion.48, pred[520]{0:T(1024)(128)(4,1)S(1)} %get-tuple-element.32, pred[1024]{0:T(1024)(128)(4,1)S(1)} %broadcast_compare_fusion, pred[520]{0:T(1024)(128)(4,1)S(1)} %get-tuple-element.33, s32[520]{0:T(1024)S(1)} %get-tuple-element.28, s32[1024]{0:T(1024)S(1)} %fusion.36, ...), kind=kLoop, calls=%fused_computation.4 | loop fusion | flops 5324800 | bytes 1077360 | tf_op jit(solution)/shard_map/convert_element_type | solution.py:105
  26.1 2.3 %select_convert_fusion.1.table_ref = bf16[1024,512]{1,0:T(8,128)(2,1)S(1)} fusion(s32[1024]{0:T(1024)S(1)} %get-tuple-element.22, s32[512]{0:T(512)S(1)} %get-tuple-element.24, s32[1024]{0:T(1024)S(1)} %get-tuple-element.23, s32[512]{0:T(512)S(1)} %get-tuple-element.25, s32[1024]{0:T(1024)S(1)} %fusion.31), kind=kLoop, calls=%fused_computation.12 | loop fusion | flops 14155776 | bytes 1064960 | tf_op jit(solution)/shard_map/convert_element_type | solution.py:53
  28.5 11.9 %all-to-all-done = bf16[32,16,1024]{2,1,0:T(8,128)(2,1)S(1)} async-done(((bf16[32,16,1024]{2,1,0:T(8,128)(2,1)}), bf16[32,16,1024]{2,1,0:T(8,128)(2,1)S(1)}, u32[]{:S(2)}, u32[]{:S(2)}) %all-to-all-start) | async-done | bytes 1048608 | tf_op jit(solution)/shard_map/all_to_all | solution.py:308
  40.4 2.7 %shard_map.55 = bf16[1024,1024]{1,0:T(8,128)(2,1)} custom-call(bf16[1024,512]{1,0:T(8,128)(2,1)S(1)} %select_convert_fusion.1.table_ref, bf16[512,1024]{1,0:T(8,128)(2,1)S(1)} %bitcast.11), custom_call_target="tpu_custom_call" | custom-call | tf_op jit(solution)/shard_map/pallas_call | solution.py:264
  43.1 0.0 copy-done.2
  43.1 4.6 %all-to-all-start.1 = ((bf16[32,32,1024]{2,1,0:T(8,128)(2,1)}), bf16[32,32,1024]{2,1,0:T(8,128)(2,1)}, u32[]{:S(2)}, u32[]{:S(2)}) async-start(bf16[32,32,1024]{2,1,0:T(8,128)(2,1)} %bitcast.2), calls=%async_computation.1 | async-start | bytes 4194304 | tf_op jit(solution)/shard_map/all_to_all | solution.py:308
  47.6 0.2 compare_or_fusion.1
  47.8 0.0 slice-start
  47.9 0.3 compare_convert_fusion.1
  48.2 0.3 slice-done
  48.5 1.2 fusion.3.odd_ref
  49.8 3.3 %fusion = (bf16[4,512,256]{2,1,0:T(8,128)(2,1)}, bf16[4,512,256]{2,1,0:T(8,128)(2,1)}) fusion(s32[512,256]{1,0:T(8,128)S(1)} %subtract_multiply_fusion.1, s32[512]{0:T(512)S(1)} %get-tuple-element.31, s32[4,256]{1,0:T(4,128)S(1)} %iota_add_fusion, pred[512,256]{1,0:T(8,128)(4,1)S(1)} %compare_or_fusion.1), kind=kLoop, calls=%fused_computation.7 | loop fusion | flops 14680064 | bytes 2758656 | tf_op jit(solution)/shard_map/convert_element_type | solution.py:30
  53.0 3.2 %fusion.1 = (bf16[4,256,512]{2,1,0:T(8,128)(2,1)}, bf16[4,256,512]{2,1,0:T(8,128)(2,1)}) fusion(s32[256,512]{1,0:T(8,128)S(1)} %subtract_multiply_fusion, s32[512]{0:T(512)S(1)} %get-tuple-element.31, s32[4,256]{1,0:T(4,128)S(1)} %iota_add_fusion, pred[256,512]{1,0:T(8,128)(4,1)S(1)} %compare_or_fusion), kind=kLoop, calls=%fused_computation.8 | loop fusion | flops 14680064 | bytes 2758656 | tf_op jit(solution)/shard_map/convert_element_type | solution.py:30
  56.2 0.0 collective-permute-done.refs_1_
  56.2 0.0 collective-permute-done.2.refs_3_
  56.2 0.1 collective-permute-done.1.refs_2_
  56.4 6.8 %filters.1 = (f32[520,1024]{1,0:T(8,128)}, f32[512,1024]{1,0:T(8,128)}) custom-call(bf16[520,1024]{1,0:T(8,128)(2,1)} %select_convert_fusion.even_ref, bf16[512,1024]{1,0:T(8,128)(2,1)} %fusion.3.odd_ref, bf16[2,256,1024]{2,1,0:T(8,128)(2,1)} %get-tuple-element.15.refs_0_, bf16[2,256,1024]{2,1,0:T(8,128)(2,1)} %collective-permute-done.refs_1_, ...), custom_call_target="tpu_custom_call" | custom-call | tf_op jit(solution)/shard_map/filters/pallas_call | solution.py:361
  63.2 12.8 %all-to-all-done.1 = bf16[32,32,1024]{2,1,0:T(8,128)(2,1)} async-done(((bf16[32,32,1024]{2,1,0:T(8,128)(2,1)}), bf16[32,32,1024]{2,1,0:T(8,128)(2,1)}, u32[]{:S(2)}, u32[]{:S(2)}) %all-to-all-start.1) | async-done | bytes 2097184 | tf_op jit(solution)/shard_map/all_to_all | solution.py:308
  76.0 19.6 %shard_map.56 = bf16[32,4,8,1024]{3,2,1,0:T(8,128)(2,1)} custom-call(bf16[4,512,256]{2,1,0:T(8,128)(2,1)} %get-tuple-element.19.mh_hbm, bf16[4,512,256]{2,1,0:T(8,128)(2,1)} %get-tuple-element.18.ml_hbm, bf16[4,256,512]{2,1,0:T(8,128)(2,1)} %get-tuple-element.17.gh_hbm, bf16[4,256,512]{2,1,0:T(8,128)(2,1)} %get-tuple-element.16.gl_hbm, ...), custom_call_target="tpu_custom_call" | custom-call | tf_op jit(solution)/shard_map/pallas_call | solution.py:264
  95.7 4.5 %all-to-all-start.2 = ((bf16[32,32,1024]{2,1,0:T(8,128)(2,1)}), bf16[32,32,1024]{2,1,0:T(8,128)(2,1)S(1)}, u32[]{:S(2)}, u32[]{:S(2)}) async-start(bf16[32,32,1024]{2,1,0:T(8,128)(2,1)} %bitcast.14), calls=%async_computation.2 | async-start | bytes 4194304 | tf_op jit(solution)/shard_map/all_to_all | solution.py:308
  100.2 2.5 %select_convert_fusion.2.table_ref = bf16[512,1024]{1,0:T(8,128)(2,1)S(1)} fusion(s32[1024]{0:T(1024)S(1)} %get-tuple-element.22, s32[1024]{0:T(1024)S(1)} %get-tuple-element.23, s32[512]{0:T(512)S(1)} %get-tuple-element.24, s32[1024]{0:T(1024)S(1)} %fusion.31, s32[512]{0:T(512)S(1)} %get-tuple-element.25), kind=kLoop, calls=%fused_computation.40 | loop fusion | flops 14155776 | bytes 1064960 | tf_op jit(solution)/shard_map/convert_element_type | solution.py:53
  102.7 25.9 %all-to-all-done.2 = bf16[32,32,1024]{2,1,0:T(8,128)(2,1)S(1)} async-done(((bf16[32,32,1024]{2,1,0:T(8,128)(2,1)}), bf16[32,32,1024]{2,1,0:T(8,128)(2,1)S(1)}, u32[]{:S(2)}, u32[]{:S(2)}) %all-to-all-start.2) | async-done | bytes 2097184 | tf_op jit(solution)/shard_map/all_to_all | solution.py:308
  128.6 1.8 %fold.1 = bf16[512,1024]{1,0:T(8,128)(2,1)S(1)} custom-call(bf16[512,1024]{1,0:T(8,128)(2,1)S(1)} %select_convert_fusion.2.table_ref, bf16[1024,1024]{1,0:T(8,128)(2,1)S(1)} %bitcast.9), custom_call_target="tpu_custom_call" | custom-call | tf_op jit(solution)/shard_map/fold/pallas_call | solution.py:282
  130.4 0.0 copy-start
  130.4 0.0 copy-start.1
  130.5 20.6 %all_to_all.20 = bf16[32,16,1024]{2,1,0:T(8,128)(2,1)S(1)} all-to-all(bf16[32,16,1024]{2,1,0:T(8,128)(2,1)S(1)} %bitcast.12), channel_id=1, replica_groups=mesh['ctx'=32,'fsdp'=4] {'ctx'}, dimensions={0} | all-to-all | bytes 2097152 | tf_op jit(solution)/shard_map/all_to_all | solution.py:308
  151.1 0.0 copy-done
  151.1 0.0 copy-done.1
  151.1 2.4 %shard_map.57 = bf16[512,1024]{1,0:T(8,128)(2,1)} custom-call(bf16[512,1024]{1,0:T(8,128)(2,1)S(1)} %bitcast.10, bf16[512,1024]{1,0:T(8,128)(2,1)} %multiply_convert_fusion.mixed_ref, bf16[512,1024]{1,0:T(8,128)(2,1)S(1)} %copy-done, f32[1,1024]{1,0:T(1,128)S(1)} %bitcast.13), custom_call_target="tpu_custom_call" | custom-call | tf_op jit(solution)/shard_map/pallas_call | solution.py:264
  (14 shorter events, 0.1 us)
Async XLA Ops:
  6.5 49.7 %collective-permute-start = (bf16[2,256,1024]{2,1,0:T(8,128)(2,1)}, bf16[2,256,1024]{2,1,0:T(8,128)(2,1)}, u32[]{:S(2)}, u32[]{:S(2)}) collective-permute-start(bf16[2,256,1024]{2,1,0:T(8,128)(2,1)} %get-tuple-element.14), channel_id=1, source_target_pairs={{0,1},{1,2},{2,3},{3,0},{4,5},{5,6},{6,7},{7,4},{8,9},{9,10},{10,1... | collective-permute-start | bytes 3145736 | tf_op jit(solution)/shard_map/ppermute | solution.py:325
  8.6 47.7 %collective-permute-start.2 = (bf16[2,256,1024]{2,1,0:T(8,128)(2,1)}, bf16[2,256,1024]{2,1,0:T(8,128)(2,1)}, u32[]{:S(2)}, u32[]{:S(2)}) collective-permute-start(bf16[2,256,1024]{2,1,0:T(8,128)(2,1)} %get-tuple-element.13), channel_id=1, source_target_pairs={{0,3},{1,0},{2,1},{3,2},{4,7},{5,4},{6,5},{7,6},{8,11},{9,8},{10,9... | collective-permute-start | bytes 3145736 | tf_op jit(solution)/shard_map/ppermute | solution.py:325
  12.1 44.3 %collective-permute-start.1 = (bf16[2,256,1024]{2,1,0:T(8,128)(2,1)}, bf16[2,256,1024]{2,1,0:T(8,128)(2,1)}, u32[]{:S(2)}, u32[]{:S(2)}) collective-permute-start(bf16[2,256,1024]{2,1,0:T(8,128)(2,1)} %constant_dynamic-slice_fusion.1), channel_id=1, source_target_pairs={{0,2},{1,3},{2,0},{3,1},{4,6},{5,7},{6,4},{7,5},{8,10},{9,11},{10,... | collective-permute-start | bytes 3145736 | tf_op jit(solution)/shard_map/ppermute | solution.py:325
  13.8 26.5 %all-to-all-start = ((bf16[32,16,1024]{2,1,0:T(8,128)(2,1)}), bf16[32,16,1024]{2,1,0:T(8,128)(2,1)S(1)}, u32[]{:S(2)}, u32[]{:S(2)}) async-start(bf16[32,16,1024]{2,1,0:T(8,128)(2,1)} %bitcast), calls=%async_computation | async-start | bytes 2097152 | tf_op jit(solution)/shard_map/all_to_all | solution.py:308
  23.5 19.6 %copy-start.2 = (f32[520]{0:T(1024)}, f32[520]{0:T(1024)S(1)}, u32[]{:S(2)}) copy-start(f32[520]{0:T(1024)S(1)} %fusion.48) | copy-start | bytes 6244
  43.1 33.0 %all-to-all-start.1 = ((bf16[32,32,1024]{2,1,0:T(8,128)(2,1)}), bf16[32,32,1024]{2,1,0:T(8,128)(2,1)}, u32[]{:S(2)}, u32[]{:S(2)}) async-start(bf16[32,32,1024]{2,1,0:T(8,128)(2,1)} %bitcast.2), calls=%async_computation.1 | async-start | bytes 4194304 | tf_op jit(solution)/shard_map/all_to_all | solution.py:308
  47.8 0.7 slice-start
  95.7 32.9 %all-to-all-start.2 = ((bf16[32,32,1024]{2,1,0:T(8,128)(2,1)}), bf16[32,32,1024]{2,1,0:T(8,128)(2,1)S(1)}, u32[]{:S(2)}, u32[]{:S(2)}) async-start(bf16[32,32,1024]{2,1,0:T(8,128)(2,1)} %bitcast.14), calls=%async_computation.2 | async-start | bytes 4194304 | tf_op jit(solution)/shard_map/all_to_all | solution.py:308
  130.4 20.7 %copy-start = (bf16[512,1024]{1,0:T(8,128)(2,1)S(1)}, bf16[512,1024]{1,0:T(8,128)(2,1)}, u32[]{:S(2)}) copy-start(bf16[512,1024]{1,0:T(8,128)(2,1)} %gate_ref.1) | copy-start | bytes 3145732
  130.4 20.7 %copy-start.1 = (f32[1024]{0:T(1024)S(1)}, f32[1024]{0:T(1024)}, u32[]{:S(2)}) copy-start(f32[1024]{0:T(1024)} %param.8) | copy-start | bytes 12292

commit v4 on v3

--- a/solution.py
+++ b/solution.py
@@ -9,7 +9,7 @@
 from jax.sharding import PartitionSpec as P
 
 
-LANES = 256
+LANES = 512
 RADIX = 4
 SPREAD = 1.624475
 
@@ -23,11 +23,6 @@
     for term in (-1.0 / 39916800.0, 1.0 / 362880.0, -1.0 / 5040.0, 1.0 / 120.0, -1.0 / 6.0, 1.0):
         series = series * z + term
     return series * y
-
-
-def split(table):
-    high = lax.reduce_precision(table, 8, 7)
-    return high.astype(jnp.bfloat16), (table - high).astype(jnp.bfloat16)
 
 
 def message(index, block):
@@ -77,7 +72,7 @@
         row = digit + base[None, None, :]
         step = row * rate[None, :, None] + quarter * (out_part[None, :, None] - in_phase[None, None, :])
         keep = (side[:, None] == 2) | (side[:, None] == in_part[None, :])
-    return split(jnp.where(keep[None], cosine(step, length), 0.0))
+    return jnp.where(keep[None], cosine(step, length), 0.0).astype(jnp.bfloat16)
 
 
 def filter_tables(position, member, members, rows):
@@ -105,14 +100,6 @@
     return even.astype(jnp.bfloat16), odd[:rows].astype(jnp.bfloat16)
 
 
-def dot(high, low, x):
-    return jnp.dot(
-        jnp.concatenate([high, low], axis=1),
-        jnp.concatenate([x, x], axis=0),
-        preferred_element_type=jnp.float32,
-    )
-
-
 def each_block(width, step):
     def go(i, carry):
         step(i, pl.ds(pl.multiple_of(i * LANES, LANES), LANES))
@@ -155,25 +142,17 @@
 
 
 def local_kernel(
-    mh_hbm, ml_hbm, gh_hbm, gl_hbm, even_hbm, odd_hbm, x_hbm, o_hbm,
-    mh_ref, ml_ref, gh_ref, gl_ref, even_ref, odd_ref, x_ref, o_ref, m_sem, g_sem, h_sem, x_sem, o_sem,
+    m_hbm, g_hbm, even_hbm, odd_hbm, x_hbm, o_hbm,
+    m_ref, g_ref, even_ref, odd_ref, x_ref, o_ref, b_ref, m_sem, g_sem, h_sem, x_sem, o_sem,
 ):
     rows, width = odd_ref.shape
     quart = rows // RADIX
 
-    def tables(sources, places, sems, digit):
-        return [
-            pltpu.make_async_copy(source.at[digit], place.at[digit], sems.at[n, digit])
-            for n, (source, place) in enumerate(zip(sources, places))
-        ]
-
-    def forward(digit):
-        return tables((mh_hbm, ml_hbm), (mh_ref, ml_ref), m_sem, digit) + [
-            pltpu.make_async_copy(x_hbm.at[:, digit], x_ref.at[:, digit], x_sem.at[digit])
-        ]
-
-    def backward(digit):
-        return tables((gh_hbm, gl_hbm), (gh_ref, gl_ref), g_sem, digit)
+    forward = pltpu.make_async_copy(m_hbm, m_ref, m_sem)
+    backward = pltpu.make_async_copy(g_hbm, g_ref, g_sem)
+
+    def incoming(i, cols):
+        return pltpu.make_async_copy(x_hbm.at[:, :, :, cols], x_ref.at[:, :, :, cols], x_sem.at[i])
 
     def filters(i, cols):
         return [
@@ -192,25 +171,24 @@
         for copy in copies:
             copy.wait()
 
-    for digit in range(RADIX):
-        start(forward(digit))
-    start(filters(0, pl.ds(0, LANES)))
-    for digit in range(RADIX):
-        start(backward(digit))
-    for i in range(1, width // LANES):
+    forward.start()
+    for i in range(width // LANES):
+        incoming(i, pl.ds(i * LANES, LANES)).start()
         start(filters(i, pl.ds(i * LANES, LANES)))
-
-    def step(i, cols):
+    backward.start()
+    forward.wait()
+
+    def ahead(i, cols):
+        incoming(i, cols).wait()
         v = []
         for digit in range(RADIX):
-            pl.when(i == 0)(lambda digit=digit: wait(forward(digit)))
             x = x_ref[:, digit, :, cols]
-            v.append(dot(mh_ref[digit], ml_ref[digit], x.reshape(-1, x.shape[-1])))
+            x = x.reshape(-1, x.shape[-1])
+            v.append(jnp.dot(m_ref[digit], x, preferred_element_type=jnp.float32))
         wait(filters(i, cols))
         sum02, sum13, gap02, gap13 = v[0] + v[2], v[1] + v[3], v[0] - v[2], v[1] - v[3]
         edge = (sum02[:8] - sum13[:8]) * even_ref[rows:, cols]
         total = sum02 + sum13
-        packed = [[] for _ in range(RADIX)]
         for group in range(2):
             at = 2 * group * quart
             re, im = slice(at, at + quart), slice(at + quart, at + 2 * quart)
@@ -227,18 +205,19 @@
             ):
                 if group == 0:
                     top = real[:8] + edge if digit % 2 == 0 else real[:8] - edge
-                    packed[digit].append(jnp.concatenate([top, real[8:]], axis=0))
-                else:
-                    packed[digit].append(real)
-                packed[digit].append(imag)
+                    real = jnp.concatenate([top, real[8:]], axis=0)
+                b_ref[digit, re, cols] = real.astype(b_ref.dtype)
+                b_ref[digit, im, cols] = imag.astype(b_ref.dtype)
+
+    def back(i, cols):
         for digit in range(RADIX):
-            pl.when(i == 0)(lambda digit=digit: wait(backward(digit)))
-            b = jnp.concatenate(packed[digit], axis=0).astype(jnp.bfloat16)
-            y = dot(gh_ref[digit], gl_ref[digit], b)
+            y = jnp.dot(g_ref[digit], b_ref[digit, :, cols], preferred_element_type=jnp.float32)
             o_ref[:, digit, :, cols] = y.reshape(o_ref.shape[0], o_ref.shape[2], -1).astype(o_ref.dtype)
         store(i, cols).start()
 
-    each_block(width, step)
+    each_block(width, ahead)
+    backward.wait()
+    each_block(width, back)
     each_block(width, lambda i, cols: store(i, cols).wait())
 
 
@@ -289,13 +268,14 @@
     )(table, x)
 
 
-def apply_local(tables, even, odd, x):
+def apply_local(forward, backward, even, odd, x):
     count = x.shape[-1] // LANES
     dma = pltpu.SemaphoreType.DMA
-    scratch = [pltpu.VMEM(t.shape, t.dtype) for t in (*tables, even, odd, x, x)]
-    scratch += [dma((2, RADIX)), dma((2, RADIX)), dma((2, count)), dma((RADIX,)), dma((count,))]
+    scratch = [pltpu.VMEM(t.shape, t.dtype) for t in (forward, backward, even, odd, x, x)]
+    scratch += [pltpu.VMEM((RADIX, odd.shape[0], odd.shape[1]), x.dtype)]
+    scratch += [dma(()), dma(()), dma((2, count)), dma((count,)), dma((count,))]
     out = jax.ShapeDtypeStruct(x.shape, x.dtype)
-    return call(local_kernel, (*tables, even, odd, x), (), out, scratch, 62)
+    return call(local_kernel, (forward, backward, even, odd, x), (), out, scratch, 62)
 
 
 def apply_gate(restored, mixed, gate_out, bias):
@@ -344,7 +324,7 @@
 
     spread = apply_cross(cross, stage.reshape(rows, channels), 1.0 / SPREAD)
     stage = exchange(spread.reshape(devices, 2 * block, channels))
-    turned = apply_local(local + local_back, even, odd, stage.reshape(devices, RADIX, -1, channels))
+    turned = apply_local(local, local_back, even, odd, stage.reshape(devices, RADIX, -1, channels))
     stage = exchange(turned.reshape(devices, 2 * block, channels))
     folded = apply_fold(cross_back, stage.reshape(2 * rows, channels), 2.0 / (length * SPREAD))
     restored = exchange(folded.reshape(devices, block, channels)).reshape(rows, channels)

time: 154 us -> 142 us (0.922)
  Pallas kernels: 33.4 us -> 20.7 us
    pallas_call x3, Pallas kernels: 24.7 us -> 13.1 us  [call(): pl.pallas_call(kernel, in_specs=[there] * len(stored) + [pl.BlockSpec(mem...]
where the time goes in v4:
time: 142 us
  waiting for transfers between devices  52.1 us (37%)
  starting transfers between devices  23.9 us (17%)
  Pallas kernels  20.7 us (15%)
  blocking collectives  20.6 us (15%)
  other arithmetic  17.8 us (13%)
  local copies, waits for them, and re-layouts  6.23 us (4%)
    all_to_all x3, waiting for transfers between devices, exchange(): return lax.all_to_all(array, 'ctx', split_axis=0, concat_axis=0, tiled=True)  51.1 us
    all_to_all x1, blocking collectives, exchange(): return lax.all_to_all(array, 'ctx', split_axis=0, concat_axis=0, tiled=True)  20.6 us
    all_to_all x3, starting transfers between devices, exchange(): return lax.all_to_all(array, 'ctx', split_axis=0, concat_axis=0, tiled=True)  18.8 us
    pallas_call x3, Pallas kernels, call(): pl.pallas_call(kernel, in_specs=[there] * len(stored) + [pl.BlockSpec(mem...  13.1 us
    pallas_call x1, Pallas kernels, filters(): pl.pallas_call(filter_kernel, grid=(channels // LANES,), in_specs=[whole(...  6.21 us
    dynamic_slice x2, local copies, waits for them, and re-layouts, piece_for(): return lax.dynamic_slice_in_dim(stored, target * channels, channels, 2)  5.89 us
    convert_element_type x2, other arithmetic, local_table(): return jnp.where(keep[None], cosine(step, length), 0.0).astype(jnp.bfloat16)  5.74 us
    ppermute x3, starting transfers between devices, send(): lax.ppermute(piece, 'fsdp', [(m, (m + shift) % members) for m in range(me...  5.03 us
  transfers between devices with their start and end apart: 6, of which 4 were waited for; matrix products, arithmetic and copies ran while one was open for 12% of the time, Pallas kernels for 6%

profile of v4, /device:TPU:1, one launch (start us, length us, event | category | flops | bytes accessed | tf_op | source)
XLA Modules:
  0.0 141.8 jit_solution(13868672326428365062)
XLA Ops:
  0.0 2.9 %multiply_convert_fusion.mixed_ref = bf16[512,1024]{1,0:T(8,128)(2,1)} fusion(bf16[512,1024]{1,0:T(8,128)(2,1)} %param.6, bf16[512,1024]{1,0:T(8,128)(2,1)} %param.5), kind=kLoop, calls=%fused_computation.15 | loop fusion | flops 2097152 | bytes 3145728 | tf_op jit(solution)/shard_map/convert_element_type | solution.py:311
  2.9 3.6 %constant_dynamic-slice_fusion = (bf16[2,256,1024]{2,1,0:T(8,128)(2,1)}, bf16[2,256,1024]{2,1,0:T(8,128)(2,1)}, bf16[2,256,1024]{2,1,0:T(8,128)(2,1)}) fusion(bf16[2,256,4096]{2,1,0:T(8,128)(2,1)} %param.9, s32[]{:T(128)S(6)} %select_n.553, s32[]{:T(128)S(6)} %select_n.551, s32[]{:T(128)S(6)} %select_n.550), kind=kLoop, calls=%fused_computation.163 | loop fusion | bytes 6291468 | tf_op jit(solution)/shard_map/dynamic_slice | solution.py:302
  6.5 2.0 %collective-permute-start = (bf16[2,256,1024]{2,1,0:T(8,128)(2,1)}, bf16[2,256,1024]{2,1,0:T(8,128)(2,1)}, u32[]{:S(2)}, u32[]{:S(2)}) collective-permute-start(bf16[2,256,1024]{2,1,0:T(8,128)(2,1)} %get-tuple-element.14), channel_id=1, source_target_pairs={{0,1},{1,2},{2,3},{3,0},{4,5},{5,6},{6,7},{7,4},{8,9},{9,10},{10,1... | collective-permute-start | bytes 3145736 | tf_op jit(solution)/shard_map/ppermute | solution.py:305
  8.6 1.3 collective-permute-start.2
  9.8 2.3 %constant_dynamic-slice_fusion.1 = bf16[2,256,1024]{2,1,0:T(8,128)(2,1)} fusion(bf16[2,256,4096]{2,1,0:T(8,128)(2,1)} %param.9, s32[]{:T(128)S(6)} %select_n.552), kind=kLoop, calls=%fused_computation.164 | loop fusion | bytes 2097156 | tf_op jit(solution)/shard_map/dynamic_slice | solution.py:302
  12.1 1.7 %collective-permute-start.1 = (bf16[2,256,1024]{2,1,0:T(8,128)(2,1)}, bf16[2,256,1024]{2,1,0:T(8,128)(2,1)}, u32[]{:S(2)}, u32[]{:S(2)}) collective-permute-start(bf16[2,256,1024]{2,1,0:T(8,128)(2,1)} %constant_dynamic-slice_fusion.1), channel_id=1, source_target_pairs={{0,2},{1,3},{2,0},{3,1},{4,6},{5,7},{6,4},{7,5},{8,10},{9,11},{10,... | collective-permute-start | bytes 3145736 | tf_op jit(solution)/shard_map/ppermute | solution.py:305
  13.9 9.6 %all-to-all-start = ((bf16[32,16,1024]{2,1,0:T(8,128)(2,1)}), bf16[32,16,1024]{2,1,0:T(8,128)(2,1)S(1)}, u32[]{:S(2)}, u32[]{:S(2)}) async-start(bf16[32,16,1024]{2,1,0:T(8,128)(2,1)} %bitcast), calls=%async_computation | async-start | bytes 2097152 | tf_op jit(solution)/shard_map/all_to_all | solution.py:288
  23.5 0.0 copy-start.2
  23.6 0.1 subtract_multiply_fusion
  23.8 0.2 compare_or_fusion
  23.9 0.1 subtract_multiply_fusion.1
  24.1 2.1 %select_convert_fusion.even_ref = bf16[520,1024]{1,0:T(8,128)(2,1)} fusion(f32[520]{0:T(1024)S(1)} %fusion.46, pred[520]{0:T(1024)(128)(4,1)S(1)} %get-tuple-element.26, pred[1024]{0:T(1024)(128)(4,1)S(1)} %broadcast_compare_fusion, pred[520]{0:T(1024)(128)(4,1)S(1)} %get-tuple-element.27, s32[520]{0:T(1024)S(1)} %get-tuple-element.24, s32[1024]{0:T(1024)S(1)} %fusion.34, ...), kind=kLoop, calls=%fused_computation | loop fusion | flops 5324800 | bytes 1077360 | tf_op jit(solution)/shard_map/convert_element_type | solution.py:100
  26.1 2.3 %select_convert_fusion.1.table_ref = bf16[1024,512]{1,0:T(8,128)(2,1)S(1)} fusion(s32[1024]{0:T(1024)S(1)} %get-tuple-element.18, s32[512]{0:T(512)S(1)} %get-tuple-element.20, s32[1024]{0:T(1024)S(1)} %get-tuple-element.19, s32[512]{0:T(512)S(1)} %get-tuple-element.21, s32[1024]{0:T(1024)S(1)} %fusion.29), kind=kLoop, calls=%fused_computation.6 | loop fusion | flops 14155776 | bytes 1064960 | tf_op jit(solution)/shard_map/convert_element_type | solution.py:48
  28.5 11.9 %all-to-all-done = bf16[32,16,1024]{2,1,0:T(8,128)(2,1)S(1)} async-done(((bf16[32,16,1024]{2,1,0:T(8,128)(2,1)}), bf16[32,16,1024]{2,1,0:T(8,128)(2,1)S(1)}, u32[]{:S(2)}, u32[]{:S(2)}) %all-to-all-start) | async-done | bytes 1048608 | tf_op jit(solution)/shard_map/all_to_all | solution.py:288
  40.4 2.5 %shard_map.55 = bf16[1024,1024]{1,0:T(8,128)(2,1)} custom-call(bf16[1024,512]{1,0:T(8,128)(2,1)S(1)} %select_convert_fusion.1.table_ref, bf16[512,1024]{1,0:T(8,128)(2,1)S(1)} %bitcast.11), custom_call_target="tpu_custom_call" | custom-call | tf_op jit(solution)/shard_map/pallas_call | solution.py:243
  42.9 0.0 copy-done.2
  42.9 4.6 %all-to-all-start.1 = ((bf16[32,32,1024]{2,1,0:T(8,128)(2,1)}), bf16[32,32,1024]{2,1,0:T(8,128)(2,1)}, u32[]{:S(2)}, u32[]{:S(2)}) async-start(bf16[32,32,1024]{2,1,0:T(8,128)(2,1)} %bitcast.2), calls=%async_computation.1 | async-start | bytes 4194304 | tf_op jit(solution)/shard_map/all_to_all | solution.py:288
  47.5 0.2 compare_or_fusion.1
  47.7 0.0 slice-start
  47.7 0.3 compare_convert_fusion.1
  48.1 0.3 slice-done
  48.4 1.3 fusion.1.odd_ref
  49.7 2.9 %select_convert_fusion.3.m_hbm = bf16[4,512,256]{2,1,0:T(8,128)(2,1)} fusion(s32[512,256]{1,0:T(8,128)S(1)} %subtract_multiply_fusion.1, s32[512]{0:T(512)S(1)} %fusion.54, s32[4,256]{1,0:T(4,128)S(1)} %iota_add_fusion, pred[512,256]{1,0:T(8,128)(4,1)S(1)} %compare_or_fusion.1), kind=kLoop, calls=%fused_computation.25 | loop fusion | flops 13107200 | bytes 1710080 | tf_op jit(solution)/shard_map/convert_element_type | solution.py:75
  52.6 2.8 %select_convert_fusion.2.g_hbm = bf16[4,256,512]{2,1,0:T(8,128)(2,1)} fusion(s32[256,512]{1,0:T(8,128)S(1)} %subtract_multiply_fusion, s32[512]{0:T(512)S(1)} %fusion.54, s32[4,256]{1,0:T(4,128)S(1)} %iota_add_fusion, pred[256,512]{1,0:T(8,128)(4,1)S(1)} %compare_or_fusion), kind=kLoop, calls=%fused_computation.16 | loop fusion | flops 13107200 | bytes 1710080 | tf_op jit(solution)/shard_map/convert_element_type | solution.py:75
  55.4 0.0 collective-permute-done.refs_1_
  55.4 0.0 collective-permute-done.2.refs_3_
  55.4 1.0 collective-permute-done.1.refs_2_
  56.4 6.2 %filters.1 = (f32[520,1024]{1,0:T(8,128)}, f32[512,1024]{1,0:T(8,128)}) custom-call(bf16[520,1024]{1,0:T(8,128)(2,1)} %select_convert_fusion.even_ref, bf16[512,1024]{1,0:T(8,128)(2,1)} %fusion.1.odd_ref, bf16[2,256,1024]{2,1,0:T(8,128)(2,1)} %get-tuple-element.15.refs_0_, bf16[2,256,1024]{2,1,0:T(8,128)(2,1)} %collective-permute-done.refs_1_, ...), custom_call_target="tpu_custom_call" | custom-call | tf_op jit(solution)/shard_map/filters/pallas_call | solution.py:341
  62.6 13.3 %all-to-all-done.1 = bf16[32,32,1024]{2,1,0:T(8,128)(2,1)} async-done(((bf16[32,32,1024]{2,1,0:T(8,128)(2,1)}), bf16[32,32,1024]{2,1,0:T(8,128)(2,1)}, u32[]{:S(2)}, u32[]{:S(2)}) %all-to-all-start.1) | async-done | bytes 2097184 | tf_op jit(solution)/shard_map/all_to_all | solution.py:288
  75.9 8.1 %shard_map.56 = bf16[32,4,8,1024]{3,2,1,0:T(8,128)(2,1)} custom-call(bf16[4,512,256]{2,1,0:T(8,128)(2,1)} %select_convert_fusion.3.m_hbm, bf16[4,256,512]{2,1,0:T(8,128)(2,1)} %select_convert_fusion.2.g_hbm, f32[520,1024]{1,0:T(8,128)} %get-tuple-element.10.even_hbm, f32[512,1024]{1,0:T(8,128)} %get-tuple-element.11.odd_hbm, ...), custom_call_target="tpu_custom_call" | custom-call | tf_op jit(solution)/shard_map/pallas_call | solution.py:243
  84.0 4.7 %all-to-all-start.2 = ((bf16[32,32,1024]{2,1,0:T(8,128)(2,1)}), bf16[32,32,1024]{2,1,0:T(8,128)(2,1)S(1)}, u32[]{:S(2)}, u32[]{:S(2)}) async-start(bf16[32,32,1024]{2,1,0:T(8,128)(2,1)} %bitcast.14), calls=%async_computation.2 | async-start | bytes 4194304 | tf_op jit(solution)/shard_map/all_to_all | solution.py:288
  88.7 2.5 %select_convert_fusion.4.table_ref = bf16[512,1024]{1,0:T(8,128)(2,1)S(1)} fusion(s32[1024]{0:T(1024)S(1)} %get-tuple-element.18, s32[1024]{0:T(1024)S(1)} %get-tuple-element.19, s32[512]{0:T(512)S(1)} %get-tuple-element.20, s32[1024]{0:T(1024)S(1)} %fusion.29, s32[512]{0:T(512)S(1)} %get-tuple-element.21), kind=kLoop, calls=%fused_computation.34 | loop fusion | flops 14155776 | bytes 1064960 | tf_op jit(solution)/shard_map/convert_element_type | solution.py:48
  91.2 25.9 %all-to-all-done.2 = bf16[32,32,1024]{2,1,0:T(8,128)(2,1)S(1)} async-done(((bf16[32,32,1024]{2,1,0:T(8,128)(2,1)}), bf16[32,32,1024]{2,1,0:T(8,128)(2,1)S(1)}, u32[]{:S(2)}, u32[]{:S(2)}) %all-to-all-start.2) | async-done | bytes 2097184 | tf_op jit(solution)/shard_map/all_to_all | solution.py:288
  117.1 1.4 %fold.1 = bf16[512,1024]{1,0:T(8,128)(2,1)S(1)} custom-call(bf16[512,1024]{1,0:T(8,128)(2,1)S(1)} %select_convert_fusion.4.table_ref, bf16[1024,1024]{1,0:T(8,128)(2,1)S(1)} %bitcast.9), custom_call_target="tpu_custom_call" | custom-call | tf_op jit(solution)/shard_map/fold/pallas_call | solution.py:261
  118.6 0.0 copy-start
  118.6 0.0 copy-start.1
  118.6 20.6 %all_to_all.20 = bf16[32,16,1024]{2,1,0:T(8,128)(2,1)S(1)} all-to-all(bf16[32,16,1024]{2,1,0:T(8,128)(2,1)S(1)} %bitcast.12), channel_id=1, replica_groups=mesh['ctx'=32,'fsdp'=4] {'ctx'}, dimensions={0} | all-to-all | bytes 2097152 | tf_op jit(solution)/shard_map/all_to_all | solution.py:288
  139.2 0.0 copy-done
  139.2 0.0 copy-done.1
  139.2 2.4 %shard_map.57 = bf16[512,1024]{1,0:T(8,128)(2,1)} custom-call(bf16[512,1024]{1,0:T(8,128)(2,1)S(1)} %bitcast.10, bf16[512,1024]{1,0:T(8,128)(2,1)} %multiply_convert_fusion.mixed_ref, bf16[512,1024]{1,0:T(8,128)(2,1)S(1)} %copy-done, f32[1,1024]{1,0:T(1,128)S(1)} %bitcast.13), custom_call_target="tpu_custom_call" | custom-call | tf_op jit(solution)/shard_map/pallas_call | solution.py:243
  (15 shorter events, 0.1 us)
Async XLA Ops:
  6.5 48.9 %collective-permute-start = (bf16[2,256,1024]{2,1,0:T(8,128)(2,1)}, bf16[2,256,1024]{2,1,0:T(8,128)(2,1)}, u32[]{:S(2)}, u32[]{:S(2)}) collective-permute-start(bf16[2,256,1024]{2,1,0:T(8,128)(2,1)} %get-tuple-element.14), channel_id=1, source_target_pairs={{0,1},{1,2},{2,3},{3,0},{4,5},{5,6},{6,7},{7,4},{8,9},{9,10},{10,1... | collective-permute-start | bytes 3145736 | tf_op jit(solution)/shard_map/ppermute | solution.py:305
  8.6 46.9 %collective-permute-start.2 = (bf16[2,256,1024]{2,1,0:T(8,128)(2,1)}, bf16[2,256,1024]{2,1,0:T(8,128)(2,1)}, u32[]{:S(2)}, u32[]{:S(2)}) collective-permute-start(bf16[2,256,1024]{2,1,0:T(8,128)(2,1)} %get-tuple-element.13), channel_id=1, source_target_pairs={{0,3},{1,0},{2,1},{3,2},{4,7},{5,4},{6,5},{7,6},{8,11},{9,8},{10,9... | collective-permute-start | bytes 3145736 | tf_op jit(solution)/shard_map/ppermute | solution.py:305
  12.1 44.3 %collective-permute-start.1 = (bf16[2,256,1024]{2,1,0:T(8,128)(2,1)}, bf16[2,256,1024]{2,1,0:T(8,128)(2,1)}, u32[]{:S(2)}, u32[]{:S(2)}) collective-permute-start(bf16[2,256,1024]{2,1,0:T(8,128)(2,1)} %constant_dynamic-slice_fusion.1), channel_id=1, source_target_pairs={{0,2},{1,3},{2,0},{3,1},{4,6},{5,7},{6,4},{7,5},{8,10},{9,11},{10,... | collective-permute-start | bytes 3145736 | tf_op jit(solution)/shard_map/ppermute | solution.py:305
  13.9 26.5 %all-to-all-start = ((bf16[32,16,1024]{2,1,0:T(8,128)(2,1)}), bf16[32,16,1024]{2,1,0:T(8,128)(2,1)S(1)}, u32[]{:S(2)}, u32[]{:S(2)}) async-start(bf16[32,16,1024]{2,1,0:T(8,128)(2,1)} %bitcast), calls=%async_computation | async-start | bytes 2097152 | tf_op jit(solution)/shard_map/all_to_all | solution.py:288
  23.5 19.4 %copy-start.2 = (f32[520]{0:T(1024)}, f32[520]{0:T(1024)S(1)}, u32[]{:S(2)}) copy-start(f32[520]{0:T(1024)S(1)} %fusion.46) | copy-start | bytes 6244
  42.9 32.9 %all-to-all-start.1 = ((bf16[32,32,1024]{2,1,0:T(8,128)(2,1)}), bf16[32,32,1024]{2,1,0:T(8,128)(2,1)}, u32[]{:S(2)}, u32[]{:S(2)}) async-start(bf16[32,32,1024]{2,1,0:T(8,128)(2,1)} %bitcast.2), calls=%async_computation.1 | async-start | bytes 4194304 | tf_op jit(solution)/shard_map/all_to_all | solution.py:288
  47.7 0.7 slice-start
  84.0 33.1 %all-to-all-start.2 = ((bf16[32,32,1024]{2,1,0:T(8,128)(2,1)}), bf16[32,32,1024]{2,1,0:T(8,128)(2,1)S(1)}, u32[]{:S(2)}, u32[]{:S(2)}) async-start(bf16[32,32,1024]{2,1,0:T(8,128)(2,1)} %bitcast.14), calls=%async_computation.2 | async-start | bytes 4194304 | tf_op jit(solution)/shard_map/all_to_all | solution.py:288
  118.6 20.7 %copy-start = (bf16[512,1024]{1,0:T(8,128)(2,1)S(1)}, bf16[512,1024]{1,0:T(8,128)(2,1)}, u32[]{:S(2)}) copy-start(bf16[512,1024]{1,0:T(8,128)(2,1)} %gate_ref.1) | copy-start | bytes 3145732
  118.6 20.7 %copy-start.1 = (f32[1024]{0:T(1024)S(1)}, f32[1024]{0:T(1024)}, u32[]{:S(2)}) copy-start(f32[1024]{0:T(1024)} %param.8) | copy-start | bytes 12292
